TPU v7x, 256 devices: a whole 4x4x8 slice. The times are simulated.
256 devices in a mesh: phi: 64 (over z, x, y_lo), row: 4 (over y_hi, core).
Axes of the slice: x: 4, y: 4 (y_hi: 2, y_lo: 2; y = y_hi * 2 + y_lo), z: 8, core: 2. Of those that a mesh axis runs over, the one named last changes fastest.
Arguments:
- density: float32 [1024, 32, 512], P('phi', None, 'row'), may hold values from 0.5 to 2
- velocity: float32 [3, 1024, 32, 512], P(None, 'phi', None, 'row'), may hold values from -0.3 to 0.3
- shifts: int32 [64], P('row'), may hold values from 0 to 255, as said below
- fractions: float32 [64], P('row'), may hold values from 0 to 1
Outputs:
- density_out: float32 [1024, 32, 512], P('phi', None, 'row')
- stepped_velocity: float32 [3, 1024, 32, 512], P(None, 'phi', None, 'row')
- image: float32 [1024, 1024], P(('phi', 'row'))
Inputs may be any that keep to these rules, and one draw needn't show every extreme that they name: `shifts`: some band has shift 0 and some band has shift 256 - 1.
All inputs are finite; a program needn't handle non-finite values.
Results may differ from a plain program's by a relative error of at most 0.000071.
Values sent between devices are 32-bit elements; how exact they have to be, the bound alone decides.
A program may use at most 64 MiB of HBM per device.

v0:
```python
import jax
import jax.numpy as jnp
from jax import lax
from jax.sharding import PartitionSpec as P

BAND = 8
STEPS = 2
NPIX = 1024


SPEED = 1.5
COURANT = 0.05
KAPPA = 1.5
R_INNER = 0.2


def padded(cells, sides, width, closed):
    for axis, dim in sides:
        count = lax.axis_size(axis)
        ends = count if closed else count - 1
        head = lax.slice_in_dim(cells, 0, width, axis=dim)
        tail = lax.slice_in_dim(cells, cells.shape[dim] - width, cells.shape[dim], axis=dim)
        cells = jnp.concatenate(
            [
                lax.ppermute(tail, axis, [(i, (i + 1) % count) for i in range(ends)]),
                cells,
                lax.ppermute(head, axis, [((i + 1) % count, i) for i in range(ends)]),
            ],
            axis=dim,
        )
    return cells


def passed_along(value, axis, steps):
    count = lax.axis_size(axis)
    pairs = [(source, (source + steps) % count) for source in range(count)]
    return lax.ppermute(value, axis, pairs)


def conserved(prim):
    rho = prim[0]
    return jnp.stack([rho, rho * prim[1], rho * prim[2], rho * prim[3]])


def divergence(extended, axis, comp):
    cons = conserved(extended)
    flux = cons * extended[comp][None]
    flux = flux.at[comp].add(extended[0])
    size = extended.shape[axis]
    low_c = lax.slice_in_dim(cons, 0, size - 1, axis=axis)
    high_c = lax.slice_in_dim(cons, 1, size, axis=axis)
    low_f = lax.slice_in_dim(flux, 0, size - 1, axis=axis)
    high_f = lax.slice_in_dim(flux, 1, size, axis=axis)
    face = 0.5 * (low_f + high_f) - 0.5 * SPEED * (high_c - low_c)
    return lax.slice_in_dim(face, 1, size - 1, axis=axis) - lax.slice_in_dim(
        face, 0, size - 2, axis=axis
    )


def advance(prim, ext_phi, padded_polar_grid, ext_radial):
    total = (
        divergence(ext_phi, 1, 2)
        + divergence(padded_polar_grid, 2, 3)
        + divergence(ext_radial, 3, 1)
    )
    fresh = conserved(prim) - COURANT * total
    rho = fresh[0]
    return jnp.stack([rho, fresh[1] / rho, fresh[2] / rho, fresh[3] / rho])


def column_light(rho, radial_index, total_radial):
    polar = rho.shape[1]
    dtau = KAPPA / polar * rho
    above = jnp.cumsum(dtau, axis=1) - dtau
    theta = (jnp.arange(polar, dtype=jnp.int32).astype(jnp.float32) + 0.5) / polar
    tilt = 1.0 + 0.5 * jnp.cos(jnp.pi * theta)
    radius = R_INNER + (radial_index.astype(jnp.float32) + 0.5) * (1.0 - R_INNER) / total_radial
    source = (1.0 / jnp.sqrt(radius))[None, None, :] * tilt[None, :, None]
    return jnp.sum(source * (1.0 - jnp.exp(-dtau)) * jnp.exp(-above), axis=1)


def pixel_corners(pixel_rows, npix, nphi, nrad):
    yy = ((pixel_rows.astype(jnp.float32) + 0.5) / npix * 2.0 - 1.0)[:, None]
    xx = ((jnp.arange(npix, dtype=jnp.int32).astype(jnp.float32) + 0.5) / npix * 2.0 - 1.0)[None, :]
    dist = jnp.sqrt(xx * xx + yy * yy)
    upos = (dist - R_INNER) / (1.0 - R_INNER) * nrad - 0.5
    radial_floor_index = jnp.floor(upos)
    radial_fraction = upos - radial_floor_index
    radial_lower_index = radial_floor_index.astype(jnp.int32)
    angle = jnp.arctan2(yy, xx)
    vpos = (angle + jnp.pi) / (2.0 * jnp.pi) * nphi - 0.5
    lfloor = jnp.floor(vpos)
    polar_fraction = vpos - lfloor
    polar_lower_index = lfloor.astype(jnp.int32) % nphi
    polar_upper_index = (polar_lower_index + 1) % nphi
    return [
        (polar_lower_index, radial_lower_index, (1.0 - polar_fraction) * (1.0 - radial_fraction)),
        (polar_upper_index, radial_lower_index, polar_fraction * (1.0 - radial_fraction)),
        (polar_lower_index, radial_lower_index + 1, (1.0 - polar_fraction) * radial_fraction),
        (polar_upper_index, radial_lower_index + 1, polar_fraction * radial_fraction),
    ]


def sample_block(table, corners, l_first, k_first):
    nl, nk = table.shape
    flat = table.reshape(-1)
    total = jnp.zeros(corners[0][2].shape, table.dtype)
    for lidx, kidx, weight in corners:
        lloc = lidx - l_first
        kloc = kidx - k_first
        valid = (lloc >= 0) & (lloc < nl) & (kloc >= 0) & (kloc < nk)
        spot = jnp.clip(lloc, 0, nl - 1) * nk + jnp.clip(kloc, 0, nk - 1)
        total = total + jnp.where(valid, weight * jnp.take(flat, spot), 0.0)
    return total


def body(density, velocity, shifts, fractions):
    cycle = lax.axis_size("phi")
    bands = lax.axis_size("row")
    cells = density.shape[0]
    radial = density.shape[2]
    nphi = cells * cycle
    nrad = radial * bands
    prim = jnp.concatenate([density[None], velocity], axis=0)
    shift_col = jnp.repeat(shifts, BAND)
    frac_col = jnp.repeat(fractions, BAND)
    whole = shift_col // cells
    remain = shift_col % cells
    levels = (cycle // 4 - 1).bit_length()
    for step in range(STEPS):
        ext_phi = padded(prim, (("phi", 1),), 1, True)
        ext_radial = padded(prim, (("row", 3),), 1, False)
        padded_polar_grid = jnp.pad(prim, ((0, 0), (0, 0), (1, 1), (0, 0)))
        prim = advance(prim, ext_phi, padded_polar_grid, ext_radial)
        for level in range(levels):
            moved = passed_along(prim, "phi", 2**level)
            taken = whole // 2**level % 2 == 1
            prim = jnp.where(taken[None, None, None, :], moved, prim)
        left = passed_along(prim, "phi", 1)
        joined = jnp.concatenate([left, prim], axis=1)
        lead = lax.slice_in_dim(joined, cells, 2 * cells, axis=1)
        trail = lax.slice_in_dim(joined, cells - 1, 2 * cells - 1, axis=1)
        for offset in range(1, cells):
            picked = (remain == offset)[None, None, None, :]
            lead = jnp.where(
                picked, lax.slice_in_dim(joined, cells - offset, 2 * cells - offset, axis=1), lead
            )
            trail = jnp.where(
                picked,
                lax.slice_in_dim(joined, cells - offset - 1, 2 * cells - offset - 1, axis=1),
                trail,
            )
        prim = (1.0 - frac_col) * lead + frac_col * trail
    radial_index = lax.axis_index("row") * radial + jnp.arange(radial, dtype=jnp.int32)
    intensity = column_light(prim[0], radial_index, nrad)
    rows_dev = NPIX // (cycle * bands)
    first_row = (lax.axis_index("phi") * bands + lax.axis_index("row")) * rows_dev
    pixel_rows = first_row + jnp.arange(rows_dev, dtype=jnp.int32)
    table = lax.all_gather(intensity, "row", axis=1, tiled=True)
    table = lax.all_gather(table, "phi", axis=0, tiled=True)
    image = sample_block(table, pixel_corners(pixel_rows, NPIX, nphi, nrad), 0, 0)
    return (prim[0], prim[1:], image)


def solution(mesh):
    in_specs = (P("phi", None, "row"), P(None, "phi", None, "row"), P("row"), P("row"))
    out_specs = (P("phi", None, "row"), P(None, "phi", None, "row"), P(("phi", "row"), None))
    return jax.shard_map(body, mesh=mesh, in_specs=in_specs, out_specs=out_specs, check_vma=False)
```

profile of v0, /device:TPU:16, one launch (start us, length us, event | category | flops | bytes accessed | tf_op | source)
XLA Modules:
  0.0 745.6 jit_solution(6598859238169226459)
XLA Ops:
  7.2 1.6 copy.28
  10.7 1.9 collective-permute-start.3
  13.7 2.4 collective-permute-start.2
  16.9 8.9 %collective-permute-start.1 = (f32[4,1,32,128]{3,1,2,0:T(1,128)}, f32[4,1,32,128]{3,1,2,0:T(1,128)S(1)}, u32[]{:S(2)}, u32[]{:S(2)}) collective-permute-start(f32[4,1,32,128]{3,1,2,0:T(1,128)} %get-tuple-element.146), channel_id=1, source_target_pairs={{4,0},{8,4},{12,8},{16,12},{20,16},{24,20},{28,24},{32,28},{36,32}... | collective-permute-start | bytes 196616 | tf_op jit(solution)/shard_map/ppermute | solution.py:27
  27.0 2.2 copy.37
  29.2 2.1 pad_maximum_fusion.2
  38.7 26.5 %collective-permute-done.4 = f32[4,16,32,128]{3,1,2,0:T(8,128)S(1)} collective-permute-done((f32[4,16,32,128]{3,1,2,0:T(8,128)S(1)}, f32[4,16,32,128]{3,1,2,0:T(8,128)S(1)}, u32[]{:S(2)}, u32[]{:S(2)}) %collective-permute-start.4) | collective-permute-done | bytes 1048608 | tf_op jit(solution)/shard_map/ppermute | solution.py:37
  65.4 26.2 %collective-permute-done.5 = f32[4,16,32,128]{3,1,2,0:T(8,128)S(1)} collective-permute-done((f32[4,16,32,128]{3,1,2,0:T(8,128)S(1)}, f32[4,16,32,128]{3,1,2,0:T(8,128)S(1)}, u32[]{:S(2)}, u32[]{:S(2)}) %collective-permute-start.5) | collective-permute-done | bytes 1048608 | tf_op jit(solution)/shard_map/ppermute | solution.py:37
  92.1 27.6 %collective-permute-done.6 = f32[4,16,32,128]{3,1,2,0:T(8,128)S(1)} collective-permute-done((f32[4,16,32,128]{3,1,2,0:T(8,128)S(1)}, f32[4,16,32,128]{3,1,2,0:T(8,128)S(1)}, u32[]{:S(2)}, u32[]{:S(2)}) %collective-permute-start.6) | collective-permute-done | bytes 1048608 | tf_op jit(solution)/shard_map/ppermute | solution.py:37
  119.9 17.4 %collective-permute-done.7 = f32[4,16,32,128]{3,1,2,0:T(8,128)S(1)} collective-permute-done((f32[4,16,32,128]{3,1,2,0:T(8,128)S(1)}, f32[4,16,32,128]{3,1,2,0:T(8,128)S(1)}, u32[]{:S(2)}, u32[]{:S(2)}) %collective-permute-start.7) | collective-permute-done | bytes 1048608 | tf_op jit(solution)/shard_map/ppermute | solution.py:37
  138.6 18.4 %collective-permute-done.8 = f32[4,16,32,128]{3,1,2,0:T(8,128)S(1)} collective-permute-done((f32[4,16,32,128]{3,1,2,0:T(8,128)S(1)}, f32[4,16,32,128]{3,1,2,0:T(8,128)S(1)}, u32[]{:S(2)}, u32[]{:S(2)}) %collective-permute-start.8) | collective-permute-done | bytes 1048608 | tf_op jit(solution)/shard_map/ppermute | solution.py:37
  157.2 3.5 multiply_add_fusion.1
  163.4 17.8 %collective-permute-start.12 = (f32[4,16,32,1]{2,1,3,0:T(8,128)S(1)}, f32[4,16,32,1]{2,1,3,0:T(8,128)}, u32[]{:S(2)}, u32[]{:S(2)}) collective-permute-start(f32[4,16,32,1]{2,1,3,0:T(8,128)S(1)} %copy.40), channel_id=1, source_target_pairs={{1,0},{2,1},{3,2},{5,4},{6,5},{7,6},{9,8},{10,9},{11,10},{13,12},{... | collective-permute-start | bytes 24584 | tf_op jit(solution)/shard_map/ppermute | solution.py:27
  182.3 1.9 collective-permute-start.11
  184.2 1.4 broadcast_multiply_fusion.4
  187.0 1.9 collective-permute-start.9
  188.9 1.3 copy.42
  190.7 2.2 copy.41
  192.9 2.1 pad_maximum_fusion.4
  200.7 28.2 %collective-permute-done.13 = f32[4,16,32,128]{3,1,2,0:T(8,128)S(1)} collective-permute-done((f32[4,16,32,128]{3,1,2,0:T(8,128)S(1)}, f32[4,16,32,128]{3,1,2,0:T(8,128)S(1)}, u32[]{:S(2)}, u32[]{:S(2)}) %collective-permute-start.13) | collective-permute-done | bytes 1048608 | tf_op jit(solution)/shard_map/ppermute | solution.py:37
  229.2 28.3 %collective-permute-done.14 = f32[4,16,32,128]{3,1,2,0:T(8,128)S(1)} collective-permute-done((f32[4,16,32,128]{3,1,2,0:T(8,128)S(1)}, f32[4,16,32,128]{3,1,2,0:T(8,128)S(1)}, u32[]{:S(2)}, u32[]{:S(2)}) %collective-permute-start.14) | collective-permute-done | bytes 1048608 | tf_op jit(solution)/shard_map/ppermute | solution.py:37
  257.7 26.4 %collective-permute-done.15 = f32[4,16,32,128]{3,1,2,0:T(8,128)S(1)} collective-permute-done((f32[4,16,32,128]{3,1,2,0:T(8,128)S(1)}, f32[4,16,32,128]{3,1,2,0:T(8,128)S(1)}, u32[]{:S(2)}, u32[]{:S(2)}) %collective-permute-start.15) | collective-permute-done | bytes 1048608 | tf_op jit(solution)/shard_map/ppermute | solution.py:37
  284.5 16.0 %collective-permute-done.16 = f32[4,16,32,128]{3,1,2,0:T(8,128)S(1)} collective-permute-done((f32[4,16,32,128]{3,1,2,0:T(8,128)S(1)}, f32[4,16,32,128]{3,1,2,0:T(8,128)S(1)}, u32[]{:S(2)}, u32[]{:S(2)}) %collective-permute-start.16) | collective-permute-done | bytes 1048608 | tf_op jit(solution)/shard_map/ppermute | solution.py:37
  300.9 18.9 %collective-permute-done.17 = f32[4,16,32,128]{3,1,2,0:T(8,128)S(1)} collective-permute-done((f32[4,16,32,128]{3,1,2,0:T(8,128)S(1)}, f32[4,16,32,128]{3,1,2,0:T(8,128)S(1)}, u32[]{:S(2)}, u32[]{:S(2)}) %collective-permute-start.17) | collective-permute-done | bytes 1048608 | tf_op jit(solution)/shard_map/ppermute | solution.py:37
  319.9 3.5 multiply_add_fusion
  323.6 19.1 %all_gather.6 = f32[16,512]{1,0:T(8,128)} all-gather(f32[16,128]{1,0:T(8,128)S(1)} %fusion.116), channel_id=1, replica_groups=mesh['phi'=64,'row'=4] {'row'}, dimensions={1}, use_global_device_ids=true | all-gather | bytes 40960 | tf_op jit(solution)/shard_map/all_gather | solution.py:159
  345.0 298.5 %all-gather.2.cloned.1.call-done = f32[1024,512]{1,0:T(8,128)} async-done(((f32[16,512]{1,0:T(8,128)}), f32[1024,512]{1,0:T(8,128)}) %all-gather.2.cloned.1.call-update) | async-done | bytes 2097168 | tf_op jit(solution)/shard_map/all_gather | solution.py:160
  643.5 2.1 copy.45
  645.7 23.0 %gather_fusion.3 = f32[4096]{0:T(1024)S(1)} fusion(f32[524288]{0:T(1024)S(1)} %bitcast.63, s32[4096]{0:T(1024)S(1)} %bitcast_clamp_fusion), kind=kCustom, calls=%fused_computation.3.clone | custom fusion | bytes 49152 | tf_op jit(solution)/shard_map/jit(_take)/gather | solution.py:113
  668.7 23.0 %gather_fusion.2 = f32[4096]{0:T(1024)S(1)} fusion(f32[524288]{0:T(1024)S(1)} %bitcast.64, s32[4096]{0:T(1024)S(1)} %bitcast_clamp_fusion.1), kind=kCustom, calls=%fused_computation.2.clone | custom fusion | bytes 49152 | tf_op jit(solution)/shard_map/jit(_take)/gather | solution.py:113
  691.8 23.0 %gather_fusion.1 = f32[4096]{0:T(1024)S(1)} fusion(f32[524288]{0:T(1024)S(1)} %bitcast.65, s32[4096]{0:T(1024)S(1)} %bitcast_clamp_fusion.2), kind=kCustom, calls=%fused_computation.1.clone | custom fusion | bytes 49152 | tf_op jit(solution)/shard_map/jit(_take)/gather | solution.py:113
  714.8 23.0 %gather_fusion = f32[4096]{0:T(1024)S(1)} fusion(f32[524288]{0:T(1024)S(1)} %bitcast.66, s32[4096]{0:T(1024)S(1)} %bitcast_clamp_fusion.3), kind=kCustom, calls=%fused_computation.clone | custom fusion | bytes 49152 | tf_op jit(solution)/shard_map/jit(_take)/gather | solution.py:113
  (185 shorter events, 29.9 us)
Async XLA Ops:
  7.2 636.4 %all-gather.2.cloned.1.call-start = ((), (), s32[]{:S(2)}) async-start(), calls=%async_computation | async-start | bytes 2129920 | tf_op jit(solution)/shard_map/all_gather | solution.py:160
  10.7 15.8 %collective-permute-start.3 = (f32[4,16,32,1]{2,1,3,0:T(8,128)S(1)}, f32[4,16,32,1]{2,1,3,0:T(8,128)S(1)}, u32[]{:S(2)}, u32[]{:S(2)}) collective-permute-start(f32[4,16,32,1]{2,1,3,0:T(8,128)S(1)} %copy.36), channel_id=1, source_target_pairs={{1,0},{2,1},{3,2},{5,4},{6,5},{7,6},{9,8},{10,9},{11,10},{13,12},{... | collective-permute-start | bytes 24584 | tf_op jit(solution)/shard_map/ppermute | solution.py:27
  13.7 13.3 %collective-permute-start.2 = (f32[4,16,32,1]{2,1,3,0:T(8,128)}, f32[4,16,32,1]{2,1,3,0:T(8,128)}, u32[]{:S(2)}, u32[]{:S(2)}) collective-permute-start(f32[4,16,32,1]{2,1,3,0:T(8,128)} %copy.35), channel_id=1, source_target_pairs={{0,1},{1,2},{2,3},{4,5},{5,6},{6,7},{8,9},{9,10},{10,11},{12,13},{... | collective-permute-start | bytes 24584 | tf_op jit(solution)/shard_map/ppermute | solution.py:25
  16.9 16.7 %collective-permute-start.1 = (f32[4,1,32,128]{3,1,2,0:T(1,128)}, f32[4,1,32,128]{3,1,2,0:T(1,128)S(1)}, u32[]{:S(2)}, u32[]{:S(2)}) collective-permute-start(f32[4,1,32,128]{3,1,2,0:T(1,128)} %get-tuple-element.146), channel_id=1, source_target_pairs={{4,0},{8,4},{12,8},{16,12},{20,16},{24,20},{28,24},{32,28},{36,32}... | collective-permute-start | bytes 196616 | tf_op jit(solution)/shard_map/ppermute | solution.py:27
  25.8 8.8 %collective-permute-start = (f32[4,1,32,128]{3,1,2,0:T(1,128)}, f32[4,1,32,128]{3,1,2,0:T(1,128)}, u32[]{:S(2)}, u32[]{:S(2)}) collective-permute-start(f32[4,1,32,128]{3,1,2,0:T(1,128)} %get-tuple-element.145), channel_id=1, source_target_pairs={{0,4},{4,8},{8,12},{12,16},{16,20},{20,24},{24,28},{28,32},{32,36}... | collective-permute-start | bytes 196616 | tf_op jit(solution)/shard_map/ppermute | solution.py:25
  37.9 27.3 %collective-permute-start.4 = (f32[4,16,32,128]{3,1,2,0:T(8,128)S(1)}, f32[4,16,32,128]{3,1,2,0:T(8,128)S(1)}, u32[]{:S(2)}, u32[]{:S(2)}) collective-permute-start(f32[4,16,32,128]{3,1,2,0:T(8,128)S(1)} %pad_maximum_fusion.14), channel_id=1, source_target_pairs={{0,4},{4,8},{8,12},{12,16},{16,20},{20,24},{24,28},{28,32},{32,36}... | collective-permute-start | bytes 3145736 | tf_op jit(solution)/shard_map/ppermute | solution.py:37
  38.7 81.0 %copy-start.8 = (pred[128]{0:T(512)(128)(4,1)}, pred[128]{0:T(512)(128)(4,1)S(1)}, u32[]{:S(2)}) copy-start(pred[128]{0:T(512)(128)(4,1)S(1)} %get-tuple-element.175) | copy-start | bytes 388
  65.3 26.3 %collective-permute-start.5 = (f32[4,16,32,128]{3,1,2,0:T(8,128)S(1)}, f32[4,16,32,128]{3,1,2,0:T(8,128)S(1)}, u32[]{:S(2)}, u32[]{:S(2)}) collective-permute-start(f32[4,16,32,128]{3,1,2,0:T(8,128)S(1)} %broadcast_select_fusion.1), channel_id=1, source_target_pairs={{0,8},{4,12},{8,16},{12,20},{16,24},{20,28},{24,32},{28,36},{32,40... | collective-permute-start | bytes 3145736 | tf_op jit(solution)/shard_map/ppermute | solution.py:37
  91.8 27.9 %collective-permute-start.6 = (f32[4,16,32,128]{3,1,2,0:T(8,128)S(1)}, f32[4,16,32,128]{3,1,2,0:T(8,128)S(1)}, u32[]{:S(2)}, u32[]{:S(2)}) collective-permute-start(f32[4,16,32,128]{3,1,2,0:T(8,128)S(1)} %broadcast_select_fusion.3), channel_id=1, source_target_pairs={{0,16},{4,20},{8,24},{12,28},{16,32},{20,36},{24,40},{28,44},{32,4... | collective-permute-start | bytes 3145736 | tf_op jit(solution)/shard_map/ppermute | solution.py:37
  119.8 17.5 %collective-permute-start.7 = (f32[4,16,32,128]{3,1,2,0:T(8,128)S(1)}, f32[4,16,32,128]{3,1,2,0:T(8,128)S(1)}, u32[]{:S(2)}, u32[]{:S(2)}) collective-permute-start(f32[4,16,32,128]{3,1,2,0:T(8,128)S(1)} %broadcast_select_fusion.5), channel_id=1, source_target_pairs={{0,32},{4,36},{8,40},{12,44},{16,48},{20,52},{24,56},{28,60},{32,6... | collective-permute-start | bytes 3145736 | tf_op jit(solution)/shard_map/ppermute | solution.py:37
  137.4 19.6 %collective-permute-start.8 = (f32[4,16,32,128]{3,1,2,0:T(8,128)S(1)}, f32[4,16,32,128]{3,1,2,0:T(8,128)S(1)}, u32[]{:S(2)}, u32[]{:S(2)}) collective-permute-start(f32[4,16,32,128]{3,1,2,0:T(8,128)S(1)} %broadcast_select_fusion.7), channel_id=1, source_target_pairs={{0,4},{4,8},{8,12},{12,16},{16,20},{20,24},{24,28},{28,32},{32,36}... | collective-permute-start | bytes 3145736 | tf_op jit(solution)/shard_map/ppermute | solution.py:37
  163.4 25.5 %collective-permute-start.12 = (f32[4,16,32,1]{2,1,3,0:T(8,128)S(1)}, f32[4,16,32,1]{2,1,3,0:T(8,128)}, u32[]{:S(2)}, u32[]{:S(2)}) collective-permute-start(f32[4,16,32,1]{2,1,3,0:T(8,128)S(1)} %copy.40), channel_id=1, source_target_pairs={{1,0},{2,1},{3,2},{5,4},{6,5},{7,6},{9,8},{10,9},{11,10},{13,12},{... | collective-permute-start | bytes 24584 | tf_op jit(solution)/shard_map/ppermute | solution.py:27
  182.3 8.4 %collective-permute-start.11 = (f32[4,16,32,1]{2,1,3,0:T(8,128)}, f32[4,16,32,1]{2,1,3,0:T(8,128)}, u32[]{:S(2)}, u32[]{:S(2)}) collective-permute-start(f32[4,16,32,1]{2,1,3,0:T(8,128)} %copy.39), channel_id=1, source_target_pairs={{0,1},{1,2},{2,3},{4,5},{5,6},{6,7},{8,9},{9,10},{10,11},{12,13},{... | collective-permute-start | bytes 24584 | tf_op jit(solution)/shard_map/ppermute | solution.py:25
  185.7 11.6 %collective-permute-start.10 = (f32[4,1,32,128]{3,1,2,0:T(1,128)}, f32[4,1,32,128]{3,1,2,0:T(1,128)S(1)}, u32[]{:S(2)}, u32[]{:S(2)}) collective-permute-start(f32[4,1,32,128]{3,1,2,0:T(1,128)} %get-tuple-element.130), channel_id=1, source_target_pairs={{4,0},{8,4},{12,8},{16,12},{20,16},{24,20},{28,24},{32,28},{36,32}... | collective-permute-start | bytes 196616 | tf_op jit(solution)/shard_map/ppermute | solution.py:27
  187.0 10.2 %collective-permute-start.9 = (f32[4,1,32,128]{3,1,2,0:T(1,128)}, f32[4,1,32,128]{3,1,2,0:T(1,128)}, u32[]{:S(2)}, u32[]{:S(2)}) collective-permute-start(f32[4,1,32,128]{3,1,2,0:T(1,128)} %get-tuple-element.129), channel_id=1, source_target_pairs={{0,4},{4,8},{8,12},{12,16},{16,20},{20,24},{24,28},{28,32},{32,36}... | collective-permute-start | bytes 196616 | tf_op jit(solution)/shard_map/ppermute | solution.py:25
  200.7 28.3 %collective-permute-start.13 = (f32[4,16,32,128]{3,1,2,0:T(8,128)S(1)}, f32[4,16,32,128]{3,1,2,0:T(8,128)S(1)}, u32[]{:S(2)}, u32[]{:S(2)}) collective-permute-start(f32[4,16,32,128]{3,1,2,0:T(8,128)S(1)} %pad_maximum_fusion.15), channel_id=1, source_target_pairs={{0,4},{4,8},{8,12},{12,16},{16,20},{20,24},{24,28},{28,32},{32,36}... | collective-permute-start | bytes 3145736 | tf_op jit(solution)/shard_map/ppermute | solution.py:37
  229.1 55.0 %copy-start.9 = (pred[128]{0:T(512)(128)(4,1)S(1)}, pred[128]{0:T(512)(128)(4,1)}, u32[]{:S(2)}) copy-start(pred[128]{0:T(512)(128)(4,1)} %copy-done.8) | copy-start | bytes 388
  229.1 28.4 %collective-permute-start.14 = (f32[4,16,32,128]{3,1,2,0:T(8,128)S(1)}, f32[4,16,32,128]{3,1,2,0:T(8,128)S(1)}, u32[]{:S(2)}, u32[]{:S(2)}) collective-permute-start(f32[4,16,32,128]{3,1,2,0:T(8,128)S(1)} %broadcast_select_fusion), channel_id=1, source_target_pairs={{0,8},{4,12},{8,16},{12,20},{16,24},{20,28},{24,32},{28,36},{32,40... | collective-permute-start | bytes 3145736 | tf_op jit(solution)/shard_map/ppermute | solution.py:37
  257.7 26.5 %collective-permute-start.15 = (f32[4,16,32,128]{3,1,2,0:T(8,128)S(1)}, f32[4,16,32,128]{3,1,2,0:T(8,128)S(1)}, u32[]{:S(2)}, u32[]{:S(2)}) collective-permute-start(f32[4,16,32,128]{3,1,2,0:T(8,128)S(1)} %broadcast_select_fusion.2), channel_id=1, source_target_pairs={{0,16},{4,20},{8,24},{12,28},{16,32},{20,36},{24,40},{28,44},{32,4... | collective-permute-start | bytes 3145736 | tf_op jit(solution)/shard_map/ppermute | solution.py:37
  284.3 35.5 %copy-start.7 = (f32[128]{0:T(128)S(1)}, f32[128]{0:T(128)}, u32[]{:S(2)}) copy-start(f32[128]{0:T(128)} %copy-done.6) | copy-start | bytes 1540
  284.3 35.5 %copy-start.11 = (pred[128]{0:T(512)(128)(4,1)S(1)}, pred[128]{0:T(512)(128)(4,1)}, u32[]{:S(2)}) copy-start(pred[128]{0:T(512)(128)(4,1)} %copy-done.10) | copy-start | bytes 388
  284.3 35.5 %copy-start.13 = (pred[128]{0:T(512)(128)(4,1)S(1)}, pred[128]{0:T(512)(128)(4,1)}, u32[]{:S(2)}) copy-start(pred[128]{0:T(512)(128)(4,1)} %copy-done.12) | copy-start | bytes 388
  284.3 35.5 %copy-start.15 = (pred[128]{0:T(512)(128)(4,1)S(1)}, pred[128]{0:T(512)(128)(4,1)}, u32[]{:S(2)}) copy-start(pred[128]{0:T(512)(128)(4,1)} %copy-done.14) | copy-start | bytes 388
  284.3 35.5 %copy-start.17 = (pred[128]{0:T(512)(128)(4,1)S(1)}, pred[128]{0:T(512)(128)(4,1)}, u32[]{:S(2)}) copy-start(pred[128]{0:T(512)(128)(4,1)} %copy-done.16) | copy-start | bytes 388
  284.3 35.5 %copy-start.19 = (pred[128]{0:T(512)(128)(4,1)S(1)}, pred[128]{0:T(512)(128)(4,1)}, u32[]{:S(2)}) copy-start(pred[128]{0:T(512)(128)(4,1)} %copy-done.18) | copy-start | bytes 388
  284.3 35.5 %copy-start.21 = (pred[128]{0:T(512)(128)(4,1)S(1)}, pred[128]{0:T(512)(128)(4,1)}, u32[]{:S(2)}) copy-start(pred[128]{0:T(512)(128)(4,1)} %copy-done.20) | copy-start | bytes 388
  284.3 35.5 %copy-start.23 = (pred[128]{0:T(512)(128)(4,1)S(1)}, pred[128]{0:T(512)(128)(4,1)}, u32[]{:S(2)}) copy-start(pred[128]{0:T(512)(128)(4,1)} %copy-done.22) | copy-start | bytes 388
  284.3 35.5 %copy-start.25 = (pred[128]{0:T(512)(128)(4,1)S(1)}, pred[128]{0:T(512)(128)(4,1)}, u32[]{:S(2)}) copy-start(pred[128]{0:T(512)(128)(4,1)} %copy-done.24) | copy-start | bytes 388
  284.4 35.5 %copy-start.27 = (pred[128]{0:T(512)(128)(4,1)S(1)}, pred[128]{0:T(512)(128)(4,1)}, u32[]{:S(2)}) copy-start(pred[128]{0:T(512)(128)(4,1)} %copy-done.26) | copy-start | bytes 388
  284.4 35.5 %copy-start.29 = (pred[128]{0:T(512)(128)(4,1)S(1)}, pred[128]{0:T(512)(128)(4,1)}, u32[]{:S(2)}) copy-start(pred[128]{0:T(512)(128)(4,1)} %copy-done.28) | copy-start | bytes 388
  284.4 16.1 %collective-permute-start.16 = (f32[4,16,32,128]{3,1,2,0:T(8,128)S(1)}, f32[4,16,32,128]{3,1,2,0:T(8,128)S(1)}, u32[]{:S(2)}, u32[]{:S(2)}) collective-permute-start(f32[4,16,32,128]{3,1,2,0:T(8,128)S(1)} %broadcast_select_fusion.4), channel_id=1, source_target_pairs={{0,32},{4,36},{8,40},{12,44},{16,48},{20,52},{24,56},{28,60},{32,6... | collective-permute-start | bytes 3145736 | tf_op jit(solution)/shard_map/ppermute | solution.py:37
  300.7 19.1 %collective-permute-start.17 = (f32[4,16,32,128]{3,1,2,0:T(8,128)S(1)}, f32[4,16,32,128]{3,1,2,0:T(8,128)S(1)}, u32[]{:S(2)}, u32[]{:S(2)}) collective-permute-start(f32[4,16,32,128]{3,1,2,0:T(8,128)S(1)} %broadcast_select_fusion.6), channel_id=1, source_target_pairs={{0,4},{4,8},{8,12},{12,16},{16,20},{20,24},{24,28},{28,32},{32,36}... | collective-permute-start | bytes 3145736 | tf_op jit(solution)/shard_map/ppermute | solution.py:37
  (29 other events, 483.1 us)
Sparse Core Ops, SparseCore 0:
  342.9 300.6 all-gather.1
where the time goes:
time: 746 us
  waiting for transfers between devices  534 us (72%)
  local copies, waits for them, and re-layouts  111 us (15%)
  starting transfers between devices  36.9 us (5%)
  other arithmetic  30 us (4%)
  blocking collectives  19.1 us (3%)
  between operations  15.2 us (2%)
    all_gather x1, waiting for transfers between devices, body(): table = lax.all_gather(table, 'phi', axis=0, tiled=True)  299 us
    ppermute x10, waiting for transfers between devices, passed_along(): return lax.ppermute(value, axis, pairs)  234 us
    gather x8, local copies, waits for them, and re-layouts, sample_block(): total = total + jnp.where(valid, weight * jnp.take(flat, spot), 0.0)  92.2 us
    ppermute x4, starting transfers between devices, padded(): lax.ppermute(head, axis, [((i + 1) % count, i) for i in range(ends)])  28.9 us
    all_gather x1, blocking collectives, body(): table = lax.all_gather(intensity, 'row', axis=1, tiled=True)  19.1 us
  transfers between devices with their start and end apart: 19, of which 13 were waited for; matrix products, arithmetic and copies ran while one was open for 3% of the time, Pallas kernels for 0%

commit v1 on v0

v1 whole, which is shorter than its diff:
```python
import functools

import jax
import jax.numpy as jnp
import numpy as np
from jax import lax
from jax.experimental import pallas as pl
from jax.experimental.pallas import tpu as pltpu
from jax.sharding import PartitionSpec as P

MESH = pl.DeviceIdType.MESH
BAND = 8
NPIX = 1024
NPHI = 1024
NR = 512
NTH = 32
KAPPA = 1.5
R_INNER = 0.2
F32 = jnp.float32
VM = pl.BlockSpec(memory_space=pltpu.VMEM)
SM = pl.BlockSpec(memory_space=pltpu.SMEM)
ANY = pl.BlockSpec(memory_space=pl.ANY)


def where_of(band, group):
    return (band % 8) * 8 + group * 2 + band // 8


def lanes():
    return lax.broadcasted_iota(jnp.int32, (8, 128), 1)


def conserved(q):
    return [q[0], q[0] * q[1], q[0] * q[2], q[0] * q[3]]


def side(q, comp, offset):
    m = q[0] * (0.5 * q[comp] + offset)
    out = [m, m * q[1], m * q[2], m * q[3]]
    out[comp] = out[comp] + 0.5 * q[0]
    return out


def updated(here, lower, upper):
    total = None
    for (comp, low), (_, high) in zip(lower, upper):
        p, m = side(low, comp, 0.75), side(high, comp, -0.75)
        part = [b - a for a, b in zip(p, m)]
        total = part if total is None else [s + t for s, t in zip(total, part)]
    new = [0.775 * c - 0.05 * t for c, t in zip(conserved(here), total)]
    inv = 1.0 / new[0]
    return [new[0], new[1] * inv, new[2] * inv, new[3] * inv]


def to_tiles_kernel(rho_ref, vel_ref, out_ref, edge_ref):
    for f in range(4):
        for g in range(4):
            src = rho_ref[:, 8 * g : 8 * g + 8, :] if f == 0 else vel_ref[f - 1, :, 8 * g : 8 * g + 8, :]
            t = src.reshape(128, 128).T
            out_ref[f, g] = t
            edge_ref[0, pl.ds(f * 4 + g, 1), :] = t[0:1, :]
            edge_ref[1, pl.ds(f * 4 + g, 1), :] = t[127:128, :]


def greet(peers):
    bar = pltpu.get_barrier_semaphore()
    for peer in peers:
        pl.semaphore_signal(bar, inc=1, device_id=peer, device_id_type=MESH)
    pl.semaphore_wait(bar, len(peers))


def first_edges_kernel(rho_ref, vel_ref, edge_ref, hphi_ref, hr_ref, ssem, rsem):
    phi, row = lax.axis_index("phi"), lax.axis_index("row")
    left, right = {"phi": lax.rem(phi + 63, 64)}, {"phi": lax.rem(phi + 1, 64)}
    below, above = {"row": lax.rem(row + 3, 4)}, {"row": lax.rem(row + 1, 4)}
    greet((left, right, below, above))

    def copy(i, src, dst, to):
        return pltpu.make_async_remote_copy(src, dst, ssem.at[i], rsem.at[i], device_id=to, device_id_type=MESH)

    copies = [
        copy(0, rho_ref.at[15], hphi_ref.at[0, 0], right),
        copy(1, vel_ref.at[:, 15], hphi_ref.at[0, pl.ds(1, 3)], right),
        copy(2, rho_ref.at[0], hphi_ref.at[1, 0], left),
        copy(3, vel_ref.at[:, 0], hphi_ref.at[1, pl.ds(1, 3)], left),
        copy(4, edge_ref.at[1], hr_ref.at[0], above),
        copy(5, edge_ref.at[0], hr_ref.at[1], below),
    ]
    for c in copies:
        c.start()
    for c in copies:
        c.wait()


def first_hydro_kernel(ends_ref, a_ref, hphi_ref, hr_ref, out_ref, pad, ht):
    has_low = (ends_ref[0] > 0).astype(F32)
    has_high = (ends_ref[1] > 0).astype(F32)
    for pair in range(2):
        x = jnp.concatenate(
            [hphi_ref[s, 2 * pair + f] for f in range(2) for s in range(2)], axis=0
        )
        ht[pair] = x.T
    for f in range(4):
        for g in range(4):
            pad[f, g, 8:136, :] = a_ref[f, g]
            pad[f, g, 7:8, :] = hr_ref[0, pl.ds(f * 4 + g, 1), :] * has_low
            pad[f, g, 136:137, :] = hr_ref[1, pl.ds(f * 4 + g, 1), :] * has_high
    lane = lanes()
    first, last = lane < 8, lane >= 120
    low_th, high_th = (lane % 8) == 0, (lane % 8) == 7

    def step(j, carry):
        base = pl.multiple_of(8 * j, 8)
        here = [[pad[f, g, pl.ds(base + 8, 8), :] for f in range(4)] for g in range(4)]
        edge = [ht[pair, pl.ds(base, 8), :] for pair in range(2)]
        for g in range(4):
            c = here[g]
            before = [pad[f, g, pl.ds(base, 16), :][7:15] for f in range(4)]
            after = [pad[f, g, pl.ds(base + 8, 16), :][1:9] for f in range(4)]
            thm, thp, phm, php = [], [], [], []
            for f in range(4):
                lo = pltpu.roll(here[g - 1][f], 121, 1) if g > 0 else jnp.zeros((8, 128), F32)
                hi = pltpu.roll(here[g + 1][f], 7, 1) if g < 3 else jnp.zeros((8, 128), F32)
                thm.append(jnp.where(low_th, lo, pltpu.roll(c[f], 1, 1)))
                thp.append(jnp.where(high_th, hi, pltpu.roll(c[f], 127, 1)))
                off = (f % 2) * 64 + g * 8
                lo = pltpu.roll(edge[f // 2], (128 - off) % 128, 1)
                hi = pltpu.roll(edge[f // 2], (120 - off - 32) % 128, 1)
                phm.append(jnp.where(first, lo, pltpu.roll(c[f], 8, 1)))
                php.append(jnp.where(last, hi, pltpu.roll(c[f], 120, 1)))
            new = updated(c, ((2, phm), (3, thm), (1, before)), ((2, php), (3, thp), (1, after)))
            d = lax.rem(j, 8) * 8 + g * 2 + j // 8
            for f in range(4):
                out_ref[d, f] = new[f]
        return carry

    lax.fori_loop(0, 16, step, 0)


def a2a_kernel(x_ref, o_ref, send_sem, recv_sem, loc_sem):
    me = lax.axis_index("phi")
    bar = pltpu.get_barrier_semaphore()

    def sig(d, c):
        pl.semaphore_signal(bar, inc=1, device_id={"phi": lax.rem(me + d, 64)}, device_id_type=MESH)
        return c

    lax.fori_loop(1, 64, sig, 0)
    pl.semaphore_wait(bar, 63)

    def copy(d):
        t = lax.rem(me + d, 64)
        return pltpu.make_async_remote_copy(
            x_ref.at[t], o_ref.at[me], send_sem.at[d], recv_sem.at[d],
            device_id={"phi": t}, device_id_type=MESH,
        )

    own = pltpu.make_async_copy(x_ref.at[me], o_ref.at[me], loc_sem)
    own.start()

    def go(i, c):
        copy(i).start()
        copy(64 - i).start()
        return c

    lax.fori_loop(1, 32, go, 0)
    copy(32).start()

    def done(d, c):
        copy(d).wait()
        return c

    lax.fori_loop(1, 64, done, 0)
    own.wait()


def all_to_all(x, cid):
    return pl.pallas_call(
        a2a_kernel,
        name="a2a",
        out_shape=jax.ShapeDtypeStruct(x.shape, x.dtype),
        in_specs=[ANY],
        out_specs=ANY,
        scratch_shapes=[pltpu.SemaphoreType.DMA((64,)), pltpu.SemaphoreType.DMA((64,)), pltpu.SemaphoreType.DMA],
        compiler_params=pltpu.CompilerParams(collective_id=cid, has_side_effects=True),
    )(x)


def advect(src, dst, ints, frac):
    whole, remain = ints[0], ints[1]
    w = frac[0]
    lane = lanes()
    one, two = 8 * remain, 8 * (remain + 1)
    two_roll = lax.rem(two, 128)
    keep_one, keep_two = lane >= one, lane >= two

    def rolled(p):
        slab = lax.rem(p + 128 - whole, 64)
        tiles = [src[slab, f] for f in range(4)]
        return [pltpu.roll(t, one, 1) for t in tiles] + [pltpu.roll(t, two_roll, 1) for t in tiles]

    def step(p, prev):
        cur = rolled(p)
        for f in range(4):
            lead = jnp.where(keep_one, cur[f], prev[f])
            trail = jnp.where(keep_two, cur[4 + f], prev[4 + f])
            dst[p, f] = (1.0 - w) * lead + w * trail
        return cur

    lax.fori_loop(0, 64, step, rolled(-1), unroll=2)


def first_advect_kernel(ints, frac, src, out, th_ref, r_ref):
    advect(src, out, ints, frac)
    lane8 = lanes() % 8

    def step(big, carry):
        for f in range(4):
            top = bottom = None
            for j in range(8):
                t = out[big * 8 + j, f]
                hi = pltpu.roll(t, (j - 7) % 128, 1)
                lo = pltpu.roll(t, j, 1)
                top = hi if top is None else jnp.where(lane8 == j, hi, top)
                bottom = lo if bottom is None else jnp.where(lane8 == j, lo, bottom)
                r_ref[0, big * 8 + j, pl.ds(f, 1), :] = t[0:1, :]
                r_ref[1, big * 8 + j, pl.ds(f, 1), :] = t[7:8, :]
            th_ref[0, big, f] = bottom
            th_ref[1, big, f] = top
        return carry

    lax.fori_loop(0, 8, step, 0)


def second_edges_kernel(th_ref, r_ref, hth_ref, hr_ref, ssem, rsem):
    phi, row = lax.axis_index("phi"), lax.axis_index("row")
    z, x, y = phi // 8, lax.rem(phi // 2, 4), lax.rem(phi, 2)
    band = row * 16 + y * 8 + z

    def at_band(b):
        j = lax.rem(b, 16)
        return {"phi": lax.rem(j, 8) * 8 + x * 2 + j // 8, "row": b // 16}

    def at_group(g):
        return {"phi": z * 8 + g * 2 + y}

    below, above = at_band(lax.rem(band + 63, 64)), at_band(lax.rem(band + 1, 64))
    left, right = at_group(lax.rem(x + 3, 4)), at_group(lax.rem(x + 1, 4))
    greet((below, above, left, right))

    def copy(i, src, dst, to):
        return pltpu.make_async_remote_copy(src, dst, ssem.at[i], rsem.at[i], device_id=to, device_id_type=MESH)

    copies = [
        copy(0, r_ref.at[1], hr_ref.at[0], above),
        copy(1, r_ref.at[0], hr_ref.at[1], below),
        copy(2, th_ref.at[1], hth_ref.at[0], right),
        copy(3, th_ref.at[0], hth_ref.at[1], left),
    ]
    for c in copies:
        c.start()
    for c in copies:
        c.wait()


def second_hydro_kernel(ints, frac, src, hth_ref, hr_ref, out, mid):
    scale = [(ints[i] > 0).astype(F32) for i in range(2, 6)]
    lane = lanes()
    sub = lax.broadcasted_iota(jnp.int32, (8, 128), 0)
    first, last = lane < 8, lane >= 120
    low_th, high_th = (lane % 8) == 0, (lane % 8) == 7
    low_r, high_r = sub == 0, sub == 7

    def step(big, carry):
        packed = [[hth_ref[s, big, f] * scale[2 + s] for f in range(4)] for s in range(2)]
        for j in range(8):
            p = big * 8 + j
            before, after = lax.rem(p + 63, 64), lax.rem(p + 1, 64)
            c = [src[p, f] for f in range(4)]
            thm, thp, phm, php, rm, rp = [], [], [], [], [], []
            for f in range(4):
                thm.append(jnp.where(low_th, pltpu.roll(packed[0][f], (-j) % 128, 1), pltpu.roll(c[f], 1, 1)))
                thp.append(jnp.where(high_th, pltpu.roll(packed[1][f], 7 - j, 1), pltpu.roll(c[f], 127, 1)))
                phm.append(jnp.where(first, pltpu.roll(src[before, f], 8, 1), pltpu.roll(c[f], 8, 1)))
                php.append(jnp.where(last, pltpu.roll(src[after, f], 120, 1), pltpu.roll(c[f], 120, 1)))
                lo = hr_ref[0, p, pl.ds(f, 1), :] * scale[0]
                hi = hr_ref[1, p, pl.ds(f, 1), :] * scale[1]
                rm.append(jnp.where(low_r, jnp.broadcast_to(lo, (8, 128)), pltpu.roll(c[f], 1, 0)))
                rp.append(jnp.where(high_r, jnp.broadcast_to(hi, (8, 128)), pltpu.roll(c[f], 7, 0)))
            new = updated(c, ((2, phm), (3, thm), (1, rm)), ((2, php), (3, thp), (1, rp)))
            for f in range(4):
                mid[p, f] = new[f]
        return carry

    lax.fori_loop(0, 8, step, 0)
    advect(mid, out, ints, frac)


def from_tiles_kernel(row_ref, src, rho_ref, vel_ref, light_ref, flat):
    for f in range(4):
        for g in range(4):
            x = jnp.concatenate([src[where_of(j, g), f] for j in range(16)], axis=0)
            t = x.T.reshape(16, 8, 128)
            if f == 0:
                rho_ref[:, 8 * g : 8 * g + 8, :] = t
                for i in range(16):
                    flat[pl.ds(i * 32 + 8 * g, 8), :] = t[i]
            else:
                vel_ref[f - 1, :, 8 * g : 8 * g + 8, :] = t
    k = row_ref[0] * 128 + lax.broadcasted_iota(jnp.int32, (16, 128), 1)
    radius = R_INNER + (k.astype(F32) + 0.5) * (1.0 - R_INNER) / NR
    base = 1.0 / jnp.sqrt(radius)
    seen = jnp.ones((16, 128), F32)
    total = jnp.zeros((16, 128), F32)
    for j in range(NTH):
        tilt = float(np.float32(1.0 + 0.5 * np.cos(np.pi * (j + 0.5) / NTH)))
        t = jnp.exp(flat[pl.ds(j, 16, stride=32), :] * (-KAPPA / NTH))
        total = total + tilt * ((1.0 - t) * seen)
        seen = seen * t
    light_ref[...] = base * total


def gather_kernel(x_ref, w_ref, ssem, rsem, loc_sem):
    phi, row = lax.axis_index("phi"), lax.axis_index("row")
    z, xy = phi // 8, lax.rem(phi, 8)
    me = xy * 4 + row
    bar = pltpu.get_barrier_semaphore()

    def plane(d):
        m = lax.rem(me + d, 32)
        return {"phi": z * 8 + m // 4, "row": lax.rem(m, 4)}

    def column(d):
        return {"phi": lax.rem(z + d, 8) * 8 + xy}

    def sig(d, c):
        pl.semaphore_signal(bar, inc=1, device_id=plane(d), device_id_type=MESH)
        return c

    lax.fori_loop(1, 32, sig, 0)
    for d in range(1, 8):
        pl.semaphore_signal(bar, inc=1, device_id=column(d), device_id_type=MESH)
    pl.semaphore_wait(bar, 38)
    mine = w_ref.at[row, z, xy]
    own = pltpu.make_async_copy(x_ref, mine, loc_sem)
    own.start()

    def up(d):
        return pltpu.make_async_remote_copy(
            x_ref, mine, ssem.at[32 + d], rsem.at[32 + d], device_id=column(d), device_id_type=MESH
        )

    for d in range(1, 8):
        up(d).start()
    for d in range(1, 8):
        up(d).wait()
    own.wait()

    def across(d):
        block = w_ref.at[row, :, xy]
        return pltpu.make_async_remote_copy(
            block, block, ssem.at[d], rsem.at[d], device_id=plane(d), device_id_type=MESH
        )

    def arrive(d):
        m = lax.rem(me + 32 - d, 32)
        block = w_ref.at[lax.rem(m, 4), :, m // 4]
        return pltpu.make_async_remote_copy(
            block, block, ssem.at[d], rsem.at[d], device_id=plane(d), device_id_type=MESH
        )

    def go(d, c):
        across(d).start()
        return c

    lax.fori_loop(1, 32, go, 0)

    def done(d, c):
        across(d).wait_send()
        arrive(d).wait_recv()
        return c

    lax.fori_loop(1, 32, done, 0)


@functools.lru_cache(maxsize=None)
def sample_plan(rows_dev):
    yy = ((np.arange(NPIX) + 0.5) / NPIX * 2.0 - 1.0)[:, None]
    xx = ((np.arange(NPIX) + 0.5) / NPIX * 2.0 - 1.0)[None, :]
    u = (np.sqrt(xx * xx + yy * yy) - R_INNER) / (1.0 - R_INNER) * NR - 0.5
    v = (np.arctan2(yy, xx) + np.pi) / (2.0 * np.pi) * NPHI - 0.5
    blocks = NPIX // rows_dev
    plans = []
    for b in range(blocks):
        plan = []
        for c in range(NPIX // 128):
            cut = np.s_[b * rows_dev : (b + 1) * rows_dev, c * 128 : (c + 1) * 128]
            uu, vv = u[cut], v[cut]
            for q in range(NR // 128):
                hit = (uu > q * 128 - 1.01) & (uu < q * 128 + 128.01)
                if hit.any():
                    lo = int(np.floor((vv[hit].min() - 0.01) / 8))
                    hi = int(np.floor((np.floor(vv[hit].max() + 0.01) + 1) / 8))
                    plan.append((c, q, lo, hi - lo + 1))
        plans.append(plan)
    most = max(len(p) for p in plans)
    table = np.zeros((blocks, most, 4), np.int32)
    for b, plan in enumerate(plans):
        table[b, : len(plan)] = plan
    return table


def geometry(first_row, rows_dev):
    rows = first_row + jnp.arange(rows_dev, dtype=jnp.int32)
    yy = ((rows.astype(F32) + 0.5) / NPIX * 2.0 - 1.0)[:, None]
    xx = ((jnp.arange(NPIX, dtype=jnp.int32).astype(F32) + 0.5) / NPIX * 2.0 - 1.0)[None, :]
    dist = jnp.sqrt(xx * xx + yy * yy)
    upos = (dist - R_INNER) / (1.0 - R_INNER) * NR - 0.5
    vpos = (jnp.arctan2(yy, xx) + jnp.pi) / (2.0 * jnp.pi) * NPHI - 0.5
    return jnp.concatenate([upos, upos], axis=0), jnp.concatenate([vpos, vpos], axis=0)


def sample_kernel(plan_ref, u_ref, v_ref, w_ref, out_ref, acc, *, most):
    acc[...] = jnp.zeros_like(acc)
    sub = lax.broadcasted_iota(jnp.int32, (8, 128), 0)

    def task(t, carry):
        chunk, q, lo, count = (plan_ref[t, i] for i in range(4))
        cols = pl.ds(pl.multiple_of(chunk * 128, 128), 128)
        u, v = u_ref[:, cols], v_ref[:, cols]
        floor = jnp.floor(u)
        part = u - floor
        k = floor.astype(jnp.int32) - q * 128 + jnp.where(sub >= 4, 1, 0)
        weight = jnp.where(sub >= 4, part, 1.0 - part)
        weight = jnp.where((k >= 0) & (k < 128), weight, 0.0)
        k = jnp.clip(k, 0, 127)

        def tiles(i, total):
            base = (lo + i) * 8
            start = pl.multiple_of(lax.rem(base + NPHI, NPHI), 8)
            block = w_ref[q, pl.ds(start, 8), :]
            shifted = v - base.astype(F32)
            for s in range(8):
                row = jnp.broadcast_to(block[s : s + 1, :], (8, 128))
                got = jnp.take_along_axis(row, k, axis=1, mode="promise_in_bounds")
                total = total + jnp.maximum(1.0 - jnp.abs(shifted - float(s)), 0.0) * got
            return total

        total = lax.fori_loop(0, count, tiles, jnp.zeros((8, 128), F32))
        acc[:, cols] = acc[:, cols] + weight * total
        return carry

    lax.fori_loop(0, most, task, 0)
    out_ref[...] = acc[0:4, :] + acc[4:8, :]


def body(density, velocity, shifts, fractions):
    phi, row = lax.axis_index("phi"), lax.axis_index("row")
    z, x, y = phi // 8, (phi // 2) % 4, phi % 2
    local = z + 8 * y
    band = row * 16 + local
    shift = lax.dynamic_index_in_dim(shifts, local, keepdims=False)
    frac = lax.dynamic_slice_in_dim(fractions, local, 1)
    flag = lambda c: c.astype(jnp.int32)
    ints = jnp.stack([shift // 16, shift % 16, flag(band > 0), flag(band < 63), flag(x > 0), flag(x < 3)])
    ends = jnp.stack([flag(row > 0), flag(row < 3)])
    sds = lambda *s: jax.ShapeDtypeStruct(s, F32)

    tiles, edge = pl.pallas_call(
        to_tiles_kernel, name="to_tiles", out_shape=(sds(4, 4, 128, 128), sds(2, 16, 128)),
        in_specs=[VM, VM], out_specs=(VM, VM),
    )(density, velocity)
    hphi, hr = pl.pallas_call(
        first_edges_kernel, name="edges_a", out_shape=(sds(2, 4, 32, 128), sds(2, 16, 128)),
        in_specs=[ANY, ANY, ANY], out_specs=(ANY, ANY),
        scratch_shapes=[pltpu.SemaphoreType.DMA((6,)), pltpu.SemaphoreType.DMA((6,))],
        compiler_params=pltpu.CompilerParams(collective_id=0, has_side_effects=True),
    )(density, velocity, edge)
    stepped = pl.pallas_call(
        first_hydro_kernel, name="hydro_a", out_shape=sds(64, 4, 8, 128),
        in_specs=[SM, VM, VM, VM], out_specs=VM,
        scratch_shapes=[pltpu.VMEM((4, 4, 144, 128), F32), pltpu.VMEM((2, 128, 128), F32)],
    )(ends, tiles, hphi, hr)
    cyc = all_to_all(stepped, 1)
    moved, th_edge, r_edge = pl.pallas_call(
        first_advect_kernel, name="advect_a",
        out_shape=(sds(64, 4, 8, 128), sds(2, 8, 4, 8, 128), sds(2, 64, 4, 128)),
        in_specs=[SM, SM, VM], out_specs=(VM, VM, VM),
    )(ints, frac, cyc)
    hth, hr2 = pl.pallas_call(
        second_edges_kernel, name="edges_b", out_shape=(sds(2, 8, 4, 8, 128), sds(2, 64, 4, 128)),
        in_specs=[ANY, ANY], out_specs=(ANY, ANY),
        scratch_shapes=[pltpu.SemaphoreType.DMA((4,)), pltpu.SemaphoreType.DMA((4,))],
        compiler_params=pltpu.CompilerParams(collective_id=2, has_side_effects=True),
    )(th_edge, r_edge)
    final = pl.pallas_call(
        second_hydro_kernel, name="hydro_b", out_shape=sds(64, 4, 8, 128),
        in_specs=[SM, SM, VM, VM, VM], out_specs=VM,
        scratch_shapes=[pltpu.VMEM((64, 4, 8, 128), F32)],
    )(ints, frac, moved, hth, hr2)
    back = all_to_all(final, 3)
    rho, vel, light = pl.pallas_call(
        from_tiles_kernel, name="from_tiles", out_shape=(sds(16, 32, 128), sds(3, 16, 32, 128), sds(16, 128)),
        in_specs=[SM, VM], out_specs=(VM, VM, VM),
        scratch_shapes=[pltpu.VMEM((512, 128), F32)],
    )(jnp.reshape(row, (1,)), back)
    table = pl.pallas_call(
        gather_kernel, name="gather", out_shape=sds(4, 8, 8, 16, 128),
        in_specs=[ANY], out_specs=ANY,
        scratch_shapes=[pltpu.SemaphoreType.DMA((40,)), pltpu.SemaphoreType.DMA((40,)), pltpu.SemaphoreType.DMA],
        compiler_params=pltpu.CompilerParams(collective_id=4, has_side_effects=True),
    )(light)
    rows_dev = 4
    spot = phi * 4 + row
    plan = sample_plan(rows_dev)
    upos, vpos = geometry(spot * rows_dev, rows_dev)
    image = pl.pallas_call(
        functools.partial(sample_kernel, most=plan.shape[1]), name="sample", out_shape=sds(4, 1024),
        in_specs=[SM, VM, VM, VM], out_specs=VM,
        scratch_shapes=[pltpu.VMEM((8, 1024), F32)],
    )(lax.dynamic_index_in_dim(jnp.asarray(plan), spot, keepdims=False), upos, vpos, table.reshape(4, 1024, 128))
    return rho, vel, image


def solution(mesh):
    in_specs = (P("phi", None, "row"), P(None, "phi", None, "row"), P("row"), P("row"))
    out_specs = (P("phi", None, "row"), P(None, "phi", None, "row"), P(("phi", "row"), None))
    return jax.shard_map(body, mesh=mesh, in_specs=in_specs, out_specs=out_specs, check_vma=False)
```

time: 746 us -> 174 us (0.23)
  the two profiles are of different devices: /device:TPU:16 before, /device:TPU:77 now
where the time goes in v1:
time: 174 us; the launch traced here: 173 us
  Pallas kernels  163 us (94%)
  local copies, waits for them, and re-layouts  4.46 us (3%)
  between operations  3.37 us (2%)
  other arithmetic  2.07 us (1%)
    pallas_call x2, Pallas kernels, all_to_all(): pl.pallas_call(a2a_kernel, name='a2a', out_shape=jax.ShapeDtypeStruct(x.s...  64.1 us
    pallas_call x1, Pallas kernels, body(): pl.pallas_call(gather_kernel, name='gather', out_shape=sds(4, 8, 8, 16, 1...  49.9 us
    pallas_call x1, Pallas kernels, body(): pl.pallas_call(functools.partial(sample_kernel, most=plan.shape[1]), name...  8.68 us
    pallas_call x1, Pallas kernels, body(): pl.pallas_call(second_hydro_kernel, name='hydro_b', out_shape=sds(64, 4,...  8.49 us
    pallas_call x1, Pallas kernels, body(): pl.pallas_call(first_edges_kernel, name='edges_a', out_shape=(sds(2, 4, 3...  8.11 us
    pallas_call x1, Pallas kernels, body(): pl.pallas_call(first_advect_kernel, name='advect_a', out_shape=(sds(64, 4...  6.71 us
    pallas_call x1, Pallas kernels, body(): pl.pallas_call(second_edges_kernel, name='edges_b', out_shape=(sds(2, 8,...  6.17 us
    pallas_call x1, Pallas kernels, body(): pl.pallas_call(first_hydro_kernel, name='hydro_a', out_shape=sds(64, 4, 8...  5.52 us

profile of v1, /device:TPU:77, one launch (start us, length us, event | category | flops | bytes accessed | tf_op | source)
XLA Modules:
  0.0 172.7 jit_solution(9457034555336178391)
XLA Ops:
  0.7 0.6 add_convert_fusion.ends_ref
  1.3 1.2 dynamic_slice.12.frac
  2.5 1.2 dynamic_slice.11
  6.4 0.6 stack.56.ints
  7.0 0.7 dynamic-slice_bitcast_fusion
  7.7 0.7 copy.8.plan_ref
  8.4 0.1 multiply_add_fusion
  8.5 0.1 multiply_add_fusion.1
  8.6 0.6 pad_maximum_fusion.u_ref
  9.2 0.6 pad_maximum_fusion.1.v_ref
  9.9 2.6 %to_tiles.1 = (f32[4,4,128,128]{3,2,1,0:T(8,128)}, f32[2,16,128]{2,1,0:T(8,128)}) custom-call(f32[16,32,128]{2,1,0:T(8,128)} %rho_ref.3, f32[3,16,32,128]{3,2,1,0:T(8,128)} %vel_ref.3), custom_call_target="tpu_custom_call" | custom-call | tf_op jit(solution)/shard_map/to_tiles/pallas_call | solution.py:469
  12.4 8.1 %edges_a.1 = (f32[2,4,32,128]{3,2,1,0:T(8,128)}, f32[2,16,128]{2,1,0:T(8,128)}) custom-call(f32[16,32,128]{2,1,0:T(8,128)} %rho_ref.3, f32[3,16,32,128]{3,2,1,0:T(8,128)} %vel_ref.3, f32[2,16,128]{2,1,0:T(8,128)} %get-tuple-element.16.edge_ref), custom_call_target="tpu_custom_call" | custom-call | tf_op jit(solution)/shard_map/edges_a/pallas_call | solution.py:473
  20.6 5.5 %hydro_a.1.x_ref = f32[64,4,8,128]{3,2,1,0:T(8,128)} custom-call(s32[2]{0:T(128)} %add_convert_fusion.ends_ref, f32[4,4,128,128]{3,2,1,0:T(8,128)} %get-tuple-element.15.a_ref, f32[2,4,32,128]{3,2,1,0:T(8,128)} %get-tuple-element.17.hphi_ref, f32[2,16,128]{2,1,0:T(8,128)} %get-tuple-element.18.hr_ref), custom_call_target="tpu_custom_call" | custom-call | tf_op jit(solution)/shard_map/hydro_a/pallas_call | solution.py:479
  26.1 33.4 %a2a.2.src = f32[64,4,8,128]{3,2,1,0:T(8,128)} custom-call(f32[64,4,8,128]{3,2,1,0:T(8,128)} %hydro_a.1.x_ref), custom_call_target="tpu_custom_call" | custom-call | tf_op jit(solution)/shard_map/a2a/pallas_call | solution.py:178
  59.5 6.7 %advect_a.1 = (f32[64,4,8,128]{3,2,1,0:T(8,128)}, f32[2,8,4,8,128]{4,3,2,1,0:T(8,128)}, f32[2,64,4,128]{3,2,1,0:T(4,128)}) custom-call(s32[6]{0:T(128)} %stack.56.ints, f32[1]{0:T(128)} %dynamic_slice.12.frac, f32[64,4,8,128]{3,2,1,0:T(8,128)} %a2a.2.src), custom_call_target="tpu_custom_call" | custom-call | tf_op jit(solution)/shard_map/advect_a/pallas_call | solution.py:485
  66.2 6.2 %edges_b.1 = (f32[2,8,4,8,128]{4,3,2,1,0:T(8,128)}, f32[2,64,4,128]{3,2,1,0:T(4,128)}) custom-call(f32[2,8,4,8,128]{4,3,2,1,0:T(8,128)} %get-tuple-element.20.th_ref, f32[2,64,4,128]{3,2,1,0:T(4,128)} %get-tuple-element.21.r_ref), custom_call_target="tpu_custom_call" | custom-call | tf_op jit(solution)/shard_map/edges_b/pallas_call | solution.py:490
  72.3 8.5 %hydro_b.1.x_ref = f32[64,4,8,128]{3,2,1,0:T(8,128)} custom-call(s32[6]{0:T(128)} %stack.56.ints, f32[1]{0:T(128)} %dynamic_slice.12.frac, f32[64,4,8,128]{3,2,1,0:T(8,128)} %get-tuple-element.19.src, f32[2,8,4,8,128]{4,3,2,1,0:T(8,128)} %get-tuple-element.22.hth_ref, f32[2,64,4,128]{3,2,1,0:T(4,128)} %get-tuple-element.23.hr_ref), custom_call_target="tpu_custom_call" | custom-call | tf_op jit(solution)/shard_map/hydro_b/pallas_call | solution.py:496
  80.8 30.8 %a2a.3.src = f32[64,4,8,128]{3,2,1,0:T(8,128)} custom-call(f32[64,4,8,128]{3,2,1,0:T(8,128)} %hydro_b.1.x_ref), custom_call_target="tpu_custom_call" | custom-call | tf_op jit(solution)/shard_map/a2a/pallas_call | solution.py:178
  111.6 2.5 %from_tiles.1 = (f32[16,32,128]{2,1,0:T(8,128)}, f32[3,16,32,128]{3,2,1,0:T(8,128)}, f32[16,128]{1,0:T(8,128)}) custom-call(s32[1]{0:T(128)} %bitcast.row_ref, f32[64,4,8,128]{3,2,1,0:T(8,128)} %a2a.3.src), custom_call_target="tpu_custom_call" | custom-call | tf_op jit(solution)/shard_map/from_tiles/pallas_call | solution.py:502
  114.1 49.9 %gather.1 = f32[4,8,8,16,128]{4,3,2,1,0:T(8,128)} custom-call(f32[16,128]{1,0:T(8,128)} %get-tuple-element.26.x_ref), custom_call_target="tpu_custom_call" | custom-call | tf_op jit(solution)/shard_map/gather/pallas_call | solution.py:507
  164.0 8.7 %sample.1 = f32[4,1024]{1,0:T(4,128)} custom-call(s32[16,4]{1,0:T(8,128)} %copy.8.plan_ref, f32[8,1024]{1,0:T(8,128)} %pad_maximum_fusion.u_ref, f32[8,1024]{1,0:T(8,128)} %pad_maximum_fusion.1.v_ref, f32[4,1024,128]{2,1,0:T(8,128)} %bitcast.13), custom_call_target="tpu_custom_call" | custom-call | tf_op jit(solution)/shard_map/sample/pallas_call | solution.py:517
  (3 shorter events, 0.0 us)

commit v2 on v1

v2 whole, which is shorter than its diff:
```python
import functools

import jax
import jax.numpy as jnp
import numpy as np
from jax import lax
from jax.experimental import pallas as pl
from jax.experimental.pallas import tpu as pltpu
from jax.sharding import PartitionSpec as P

MESH = pl.DeviceIdType.MESH
BAND = 8
NPIX = 1024
NPHI = 1024
NR = 512
NTH = 32
KAPPA = 1.5
R_INNER = 0.2
F32 = jnp.float32
VM = pl.BlockSpec(memory_space=pltpu.VMEM)
SM = pl.BlockSpec(memory_space=pltpu.SMEM)
ANY = pl.BlockSpec(memory_space=pl.ANY)


def where_of(band, group):
    return (band % 8) * 8 + group * 2 + band // 8


def lanes():
    return lax.broadcasted_iota(jnp.int32, (8, 128), 1)


def conserved(q):
    return [q[0], q[0] * q[1], q[0] * q[2], q[0] * q[3]]


def side(q, comp, offset):
    m = q[0] * (0.5 * q[comp] + offset)
    out = [m, m * q[1], m * q[2], m * q[3]]
    out[comp] = out[comp] + 0.5 * q[0]
    return out


def updated(here, lower, upper):
    total = None
    for (comp, low), (_, high) in zip(lower, upper):
        p, m = side(low, comp, 0.75), side(high, comp, -0.75)
        part = [b - a for a, b in zip(p, m)]
        total = part if total is None else [s + t for s, t in zip(total, part)]
    new = [0.775 * c - 0.05 * t for c, t in zip(conserved(here), total)]
    inv = 1.0 / new[0]
    return [new[0], new[1] * inv, new[2] * inv, new[3] * inv]


def spread(i):
    return jnp.where(i % 2 == 0, 4 + i // 2, 4 - (i + 1) // 2)


def position():
    phi, row = lax.axis_index("phi"), lax.axis_index("row")
    return phi, row, phi // 8, lax.rem(phi // 2, 4), lax.rem(phi, 2)


def signal(peer):
    pl.semaphore_signal(pltpu.get_barrier_semaphore(), inc=1, device_id=peer, device_id_type=MESH)


def signal_cycle(phi):
    def sig(d, c):
        signal({"phi": lax.rem(phi + d, 64)})
        return c

    lax.fori_loop(1, 64, sig, 0)


def remote(src, dst, ssem, rsem, to):
    return pltpu.make_async_remote_copy(src, dst, ssem, rsem, device_id=to, device_id_type=MESH)


def first_kernel(rho_ref, vel_ref, out_ref, pad, edge, hphi, hr, ht, stepped, essem, ersem, ssem, rsem, lsem):
    phi, row, z, _, _ = position()
    left, right = {"phi": lax.rem(phi + 63, 64)}, {"phi": lax.rem(phi + 1, 64)}
    below, above = {"row": lax.rem(row + 3, 4)}, {"row": lax.rem(row + 1, 4)}
    signal_cycle(phi)
    signal(below)
    signal(above)
    for f in range(4):
        for g in range(4):
            src = rho_ref[:, 8 * g : 8 * g + 8, :] if f == 0 else vel_ref[f - 1, :, 8 * g : 8 * g + 8, :]
            t = src.reshape(128, 128).T
            pad[f, g, 8:136, :] = t
            edge[0, pl.ds(f * 4 + g, 1), :] = t[0:1, :]
            edge[1, pl.ds(f * 4 + g, 1), :] = t[127:128, :]
    pl.semaphore_wait(pltpu.get_barrier_semaphore(), 65)
    copies = [
        remote(rho_ref.at[15], hphi.at[0, 0], essem.at[0], ersem.at[0], right),
        remote(vel_ref.at[:, 15], hphi.at[0, pl.ds(1, 3)], essem.at[1], ersem.at[1], right),
        remote(rho_ref.at[0], hphi.at[1, 0], essem.at[2], ersem.at[2], left),
        remote(vel_ref.at[:, 0], hphi.at[1, pl.ds(1, 3)], essem.at[3], ersem.at[3], left),
        remote(edge.at[1], hr.at[0], essem.at[4], ersem.at[4], above),
        remote(edge.at[0], hr.at[1], essem.at[5], ersem.at[5], below),
    ]
    for c in copies:
        c.start()
    for c in copies:
        c.wait()
    has_low = jnp.where(row > 0, 1.0, 0.0)
    has_high = jnp.where(row < 3, 1.0, 0.0)
    for pair in range(2):
        ht[pair] = jnp.concatenate([hphi[s, 2 * pair + f] for f in range(2) for s in range(2)], axis=0).T
    for f in range(4):
        for g in range(4):
            pad[f, g, 7:8, :] = hr[0, pl.ds(f * 4 + g, 1), :] * has_low
            pad[f, g, 136:137, :] = hr[1, pl.ds(f * 4 + g, 1), :] * has_high
    lane = lanes()
    first, last = lane < 8, lane >= 120
    low_th, high_th = (lane % 8) == 0, (lane % 8) == 7

    def band_at(i):
        return lax.rem(z + spread(i // 2), 8) + 8 * (i % 2)

    def spot(i, g):
        j = band_at(i)
        return lax.rem(j, 8) * 8 + g * 2 + j // 8

    def message(d):
        off = lax.rem(d - phi + 64, 64)
        return remote(stepped.at[d], out_ref.at[phi], ssem.at[off], rsem.at[off], {"phi": d})

    own = pltpu.make_async_copy(stepped.at[phi], out_ref.at[phi], lsem)

    def send(i):
        for g in range(4):
            d = spot(i, g)

            @pl.when(d != phi)
            def _():
                message(d).start()

            @pl.when(d == phi)
            def _():
                own.start()

    def step(i, carry):
        j = band_at(i)
        base = pl.multiple_of(8 * j, 8)
        here = [[pad[f, g, pl.ds(base + 8, 8), :] for f in range(4)] for g in range(4)]
        side_edge = [ht[pair, pl.ds(base, 8), :] for pair in range(2)]
        for g in range(4):
            c = here[g]
            before = [pad[f, g, pl.ds(base, 16), :][7:15] for f in range(4)]
            after = [pad[f, g, pl.ds(base + 8, 16), :][1:9] for f in range(4)]
            thm, thp, phm, php = [], [], [], []
            for f in range(4):
                lo = pltpu.roll(here[g - 1][f], 121, 1) if g > 0 else jnp.zeros((8, 128), F32)
                hi = pltpu.roll(here[g + 1][f], 7, 1) if g < 3 else jnp.zeros((8, 128), F32)
                thm.append(jnp.where(low_th, lo, pltpu.roll(c[f], 1, 1)))
                thp.append(jnp.where(high_th, hi, pltpu.roll(c[f], 127, 1)))
                off = (f % 2) * 64 + g * 8
                lo = pltpu.roll(side_edge[f // 2], (128 - off) % 128, 1)
                hi = pltpu.roll(side_edge[f // 2], (120 - off - 32) % 128, 1)
                phm.append(jnp.where(first, lo, pltpu.roll(c[f], 8, 1)))
                php.append(jnp.where(last, hi, pltpu.roll(c[f], 120, 1)))
            new = updated(c, ((2, phm), (3, thm), (1, before)), ((2, php), (3, thp), (1, after)))
            d = spot(i, g)
            for f in range(4):
                stepped[d, f] = new[f]

        @pl.when(i > 0)
        def _():
            send(i - 1)

        return carry

    lax.fori_loop(0, 16, step, 0)
    send(15)

    def done(off, c):
        message(lax.rem(phi + off, 64)).wait()
        return c

    lax.fori_loop(1, 64, done, 0)
    own.wait()


def second_kernel(
    shift_ref, frac_ref, cyc, back, table, rho_back,
    t1, th_edge, r_edge, hth, hr, fin, flat, light,
    essem, ersem, rs, rr, vs, vr, ls, us, ur, ps, prs, ss, sr, hs, hrs,
):
    phi, row, z, x, y = position()
    half, zl, xy = z // 4, lax.rem(z, 4), lax.rem(phi, 8)
    core, yh = lax.rem(row, 2), row // 2
    band = row * 16 + y * 8 + z

    def at_band(b):
        j = lax.rem(b, 16)
        return {"phi": lax.rem(j, 8) * 8 + x * 2 + j // 8, "row": b // 16}

    def at_group(g):
        return {"phi": z * 8 + g * 2 + y}

    def chip(n):
        m = lax.rem(xy * 2 + yh + n, 16)
        return {"phi": z * 8 + m // 2, "row": lax.rem(m, 2) * 2 + core}

    sibling = {"row": yh * 2 + 1 - core}
    below, above = at_band(lax.rem(band + 63, 64)), at_band(lax.rem(band + 1, 64))
    left, right = at_group(lax.rem(x + 3, 4)), at_group(lax.rem(x + 1, 4))
    signal_cycle(phi)
    for peer in (below, above, sibling):
        signal(peer)
    for n in range(1, 16):
        signal(chip(n))

    local = z + 8 * y
    shift = shift_ref[local]
    w = frac_ref[local]
    whole, remain = shift // 16, shift % 16
    lane = lanes()
    lane8 = lane % 8
    one, two = 8 * remain, 8 * (remain + 1)
    two_roll = lax.rem(two, 128)
    keep_one, keep_two = lane >= one, lane >= two

    def turn(tiles):
        return [pltpu.roll(t, one, 1) for t in tiles] + [pltpu.roll(t, two_roll, 1) for t in tiles]

    def blend(cur, prev):
        out = []
        for f in range(4):
            lead = jnp.where(keep_one, cur[f], prev[f])
            trail = jnp.where(keep_two, cur[4 + f], prev[4 + f])
            out.append((1.0 - w) * lead + w * trail)
        return out

    def cycle_slab(p):
        slab = lax.rem(p + 128 - whole, 64)
        return turn([cyc[slab, f] for f in range(4)])

    def move(big, prev):
        top, bottom = [None] * 4, [None] * 4
        for j in range(8):
            cur = cycle_slab(big * 8 + j)
            out = blend(cur, prev)
            prev = cur
            for f in range(4):
                t = out[f]
                t1[big * 8 + j, f] = t
                hi = pltpu.roll(t, (j - 7) % 128, 1)
                lo = pltpu.roll(t, j, 1)
                top[f] = hi if j == 0 else jnp.where(lane8 == j, hi, top[f])
                bottom[f] = lo if j == 0 else jnp.where(lane8 == j, lo, bottom[f])
                r_edge[0, big * 8 + j, pl.ds(f, 1), :] = t[0:1, :]
                r_edge[1, big * 8 + j, pl.ds(f, 1), :] = t[7:8, :]
        for f in range(4):
            th_edge[0, big, f] = bottom[f]
            th_edge[1, big, f] = top[f]
        return prev

    lax.fori_loop(0, 8, move, cycle_slab(-1))

    pl.semaphore_wait(pltpu.get_barrier_semaphore(), 81)
    copies = [
        remote(r_edge.at[1], hr.at[0], essem.at[0], ersem.at[0], above),
        remote(r_edge.at[0], hr.at[1], essem.at[1], ersem.at[1], below),
        remote(th_edge.at[1], hth.at[0], essem.at[2], ersem.at[2], right),
        remote(th_edge.at[0], hth.at[1], essem.at[3], ersem.at[3], left),
    ]
    for c in copies:
        c.start()
    for c in copies:
        c.wait()

    on = [jnp.where(c, 1.0, 0.0) for c in (band > 0, band < 63, x > 0, x < 3)]
    sub = lax.broadcasted_iota(jnp.int32, (8, 128), 0)
    first, last = lane < 8, lane >= 120
    low_th, high_th = lane8 == 0, lane8 == 7
    low_r, high_r = sub == 0, sub == 7

    def hydro_slab(p):
        q = lax.rem(p + 128 - whole, 64)
        before, after = lax.rem(q + 63, 64), lax.rem(q + 1, 64)
        big, j = q // 8, lax.rem(q, 8)
        back_by = lax.rem(128 - j, 128)
        c = [t1[q, f] for f in range(4)]
        thm, thp, phm, php, rm, rp = [], [], [], [], [], []
        for f in range(4):
            thm.append(jnp.where(low_th, pltpu.roll(hth[0, big, f] * on[2], back_by, 1), pltpu.roll(c[f], 1, 1)))
            thp.append(jnp.where(high_th, pltpu.roll(hth[1, big, f] * on[3], 7 - j, 1), pltpu.roll(c[f], 127, 1)))
            phm.append(jnp.where(first, pltpu.roll(t1[before, f], 8, 1), pltpu.roll(c[f], 8, 1)))
            php.append(jnp.where(last, pltpu.roll(t1[after, f], 120, 1), pltpu.roll(c[f], 120, 1)))
            lo = hr[0, q, pl.ds(f, 1), :] * on[0]
            hi = hr[1, q, pl.ds(f, 1), :] * on[1]
            rm.append(jnp.where(low_r, jnp.broadcast_to(lo, (8, 128)), pltpu.roll(c[f], 1, 0)))
            rp.append(jnp.where(high_r, jnp.broadcast_to(hi, (8, 128)), pltpu.roll(c[f], 7, 0)))
        new = updated(c, ((2, phm), (3, thm), (1, rm)), ((2, php), (3, thp), (1, rp)))
        return turn(new)

    def rho_message(p):
        off = lax.rem(p - phi + 64, 64)
        return remote(fin.at[p, 0], rho_back.at[phi], rs.at[off], rr.at[off], {"phi": p})

    def vel_message(p):
        off = lax.rem(p - phi + 64, 64)
        return remote(fin.at[p, pl.ds(1, 3)], back.at[phi], vs.at[off], vr.at[off], {"phi": p})

    own_rho = pltpu.make_async_copy(fin.at[phi, 0], rho_back.at[phi], ls.at[0])
    own_vel = pltpu.make_async_copy(fin.at[phi, pl.ds(1, 3)], back.at[phi], ls.at[1])

    def send(zoff, message, own):
        def one_slab(i, c):
            p = lax.rem(z + zoff, 8) * 8 + i

            @pl.when(p != phi)
            def _():
                message(p).start()

            @pl.when(p == phi)
            def _():
                own.start()

            return c

        lax.fori_loop(0, 8, one_slab, 0)

    def block(i, carry):
        start = lax.rem(z + spread(i), 8) * 8

        def slab(k, prev):
            cur = hydro_slab(start + k)
            out = blend(cur, prev)
            for f in range(4):
                fin[start + k, f] = out[f]
            return cur

        lax.fori_loop(0, 8, slab, hydro_slab(start - 1))

        @pl.when(i > 0)
        def _():
            send(spread(i - 1), rho_message, own_rho)

        return carry

    lax.fori_loop(0, 8, block, 0)
    send(0, rho_message, own_rho)
    send(4, vel_message, own_vel)

    def rho_done(off, c):
        rho_message(lax.rem(phi + off, 64)).wait()
        return c

    lax.fori_loop(1, 64, rho_done, 0)
    own_rho.wait()
    for g in range(4):
        t = jnp.concatenate([rho_back[where_of(j, g)] for j in range(16)], axis=0).T.reshape(16, 8, 128)
        for i in range(16):
            flat[pl.ds(i * 32 + 8 * g, 8), :] = t[i]
    k = row * 128 + lax.broadcasted_iota(jnp.int32, (16, 128), 1)
    radius = R_INNER + (k.astype(F32) + 0.5) * (1.0 - R_INNER) / NR
    seen = jnp.ones((16, 128), F32)
    total = jnp.zeros((16, 128), F32)
    for j in range(NTH):
        tilt = float(np.float32(1.0 + 0.5 * np.cos(np.pi * (j + 0.5) / NTH)))
        t = jnp.exp(flat[pl.ds(j, 16, stride=32), :] * (-KAPPA / NTH))
        total = total + tilt * ((1.0 - t) * seen)
        seen = seen * t
    light[...] = (1.0 / jnp.sqrt(radius)) * total

    slot = zl * 8 + xy + 1
    own_light = pltpu.make_async_copy(light, table.at[row, slot], ls.at[2])
    own_light.start()

    def up(n, far, dst):
        return remote(
            light, table.at[row, dst], us.at[far * 4 + n], ur.at[far * 4 + n],
            {"phi": ((half + far) % 2 * 4 + lax.rem(zl + n, 4)) * 8 + xy},
        )

    low_end, high_end = (xy == 0) & (zl == 0), (xy == 7) & (zl == 3)
    for n in range(1, 4):
        up(n, 0, slot).start()
    for cond, dst in ((low_end, 33), (high_end, 0)):

        @pl.when(cond)
        def _(dst=dst):
            for n in range(4):
                up(n, 1, dst).start()

    send(3, vel_message, own_vel)
    send(5, vel_message, own_vel)
    for n in range(1, 4):
        up(n, 0, slot).wait()
    own_light.wait()
    for end, cond, dst in ((0, low_end, 33), (3, high_end, 0)):

        @pl.when(cond)
        def _(dst=dst):
            for n in range(4):
                up(n, 1, dst).wait_send()

        for pos in range(4):

            @pl.when((xy == (0 if end == 0 else 7)) & (zl == pos))
            def _(pos=pos, end=end, dst=dst):
                up((pos - end) % 4, 1, dst).wait_recv()

    def main_copy(q, pos, ssem, rsem, to):
        return [
            remote(table.at[q, 1 + 8 * b + pos], table.at[q, 1 + 8 * b + pos], ssem.at[b], rsem.at[b], to)
            for b in range(4)
        ]

    def end_copy(q, dst, ssem, rsem, to):
        return remote(table.at[q, dst], table.at[q, dst], ssem, rsem, to)

    def to_chip(n, c):
        to = chip(n)
        for cp in main_copy(row, xy, ps.at[n], prs.at[n], to):
            cp.start()
        for pos, dst in ((0, 33), (7, 0)):

            @pl.when(xy == pos)
            def _(dst=dst):
                end_copy(row, dst, hs.at[n], hrs.at[n], to).start()

        return c

    def give(q, pos, n):
        for cp in main_copy(q, pos, ss.at[n], sr.at[n], sibling):
            cp.start()
        for at, dst in ((0, 33), (7, 0)):

            @pl.when(pos == at)
            def _(dst=dst):
                end_copy(q, dst, hs.at[16 + n], hrs.at[16 + n], sibling).start()

    lax.fori_loop(1, 16, to_chip, 0)
    give(row, xy, 0)
    for off in (2, 6, 1, 7, 0):
        send(off, vel_message, own_vel)

    def source(n):
        m = lax.rem(xy * 2 + yh + 16 - n, 16)
        return m // 2, lax.rem(m, 2)

    def from_chip(n, c):
        pos, high = source(n)
        q = high * 2 + core
        for cp in main_copy(q, pos, ps.at[n], prs.at[n], chip(n)):
            cp.wait_recv()
        for at, dst in ((0, 33), (7, 0)):

            @pl.when(pos == at)
            def _(dst=dst):
                end_copy(q, dst, hs.at[n], hrs.at[n], chip(n)).wait_recv()

        give(q, pos, n)
        return c

    lax.fori_loop(1, 16, from_chip, 0)

    def finish(n, c):
        pos, high = source(n)
        q = high * 2 + core
        other = high * 2 + 1 - core
        for cp in main_copy(q, pos, ss.at[n], sr.at[n], sibling):
            cp.wait_send()
        for cp in main_copy(other, pos, ss.at[n], sr.at[n], sibling):
            cp.wait_recv()
        for at, dst in ((0, 33), (7, 0)):

            @pl.when(pos == at)
            def _(dst=dst):
                end_copy(q, dst, hs.at[16 + n], hrs.at[16 + n], sibling).wait_send()
                end_copy(other, dst, hs.at[16 + n], hrs.at[16 + n], sibling).wait_recv()

        return c

    lax.fori_loop(0, 16, finish, 0)

    def sent(n, c):
        for cp in main_copy(row, xy, ps.at[n], prs.at[n], chip(n)):
            cp.wait_send()
        for at, dst in ((0, 33), (7, 0)):

            @pl.when(xy == at)
            def _(dst=dst):
                end_copy(row, dst, hs.at[n], hrs.at[n], chip(n)).wait_send()

        return c

    lax.fori_loop(1, 16, sent, 0)

    def vel_done(off, c):
        vel_message(lax.rem(phi + off, 64)).wait()
        return c

    lax.fori_loop(1, 64, vel_done, 0)
    own_vel.wait()


@functools.lru_cache(maxsize=None)
def sample_plan(rows_dev):
    yy = ((np.arange(NPIX) + 0.5) / NPIX * 2.0 - 1.0)[:, None]
    xx = ((np.arange(NPIX) + 0.5) / NPIX * 2.0 - 1.0)[None, :]
    u = (np.sqrt(xx * xx + yy * yy) - R_INNER) / (1.0 - R_INNER) * NR - 0.5
    v = (np.arctan2(yy, xx) + np.pi) / (2.0 * np.pi) * NPHI - 0.5
    blocks = NPIX // rows_dev
    plans = []
    for b in range(blocks):
        plan = []
        for c in range(NPIX // 128):
            cut = np.s_[b * rows_dev : (b + 1) * rows_dev, c * 128 : (c + 1) * 128]
            uu, vv = u[cut], v[cut]
            for q in range(NR // 128):
                hit = (uu > q * 128 - 1.01) & (uu < q * 128 + 128.01)
                if hit.any():
                    lo = int(np.floor((vv[hit].min() - 0.01) / 8))
                    hi = int(np.floor((np.floor(vv[hit].max() + 0.01) + 1) / 8))
                    plan.append((c, q, lo, hi - lo + 1))
        plans.append(plan)
    most = max(len(p) for p in plans)
    table = np.zeros((blocks, most, 4), np.int32)
    for b, plan in enumerate(plans):
        table[b, : len(plan)] = plan
    return table


def last_kernel(plan_ref, u_ref, v_ref, rho_src, vel_src, w_ref, rho_ref, vel_ref, out_ref, acc, *, most):
    phi, row = lax.axis_index("phi"), lax.axis_index("row")
    for f in range(4):
        for g in range(4):
            x = jnp.concatenate(
                [rho_src[where_of(j, g)] if f == 0 else vel_src[where_of(j, g), f - 1] for j in range(16)], axis=0
            )
            t = x.T.reshape(16, 8, 128)
            if f == 0:
                rho_ref[:, 8 * g : 8 * g + 8, :] = t
            else:
                vel_ref[f - 1, :, 8 * g : 8 * g + 8, :] = t
    spot = phi * 4 + row
    first_tile = phi // 32 * 64 - 2
    acc[...] = jnp.zeros_like(acc)
    sub = lax.broadcasted_iota(jnp.int32, (8, 128), 0)

    def task(t, carry):
        word = plan_ref[spot * most + t]
        chunk, q = word % 8, word // 8 % 4
        lo, count = word // 32 % 256 - 1, word // 8192
        cols = pl.ds(pl.multiple_of(chunk * 128, 128), 128)
        u, v = u_ref[:, cols], v_ref[:, cols]
        floor = jnp.floor(u)
        part = u - floor
        k = floor.astype(jnp.int32) - q * 128 + jnp.where(sub >= 4, 1, 0)
        weight = jnp.where(sub >= 4, part, 1.0 - part)
        weight = jnp.where((k >= 0) & (k < 128), weight, 0.0)
        k = jnp.clip(k, 0, 127)

        def tiles(i, total):
            base = (lo + i) * 8
            start = pl.multiple_of((lo + i - first_tile) * 8, 8)
            block = w_ref[q, pl.ds(start, 8), :]
            shifted = v - base.astype(F32)
            for s in range(8):
                line = jnp.broadcast_to(block[s : s + 1, :], (8, 128))
                got = jnp.take_along_axis(line, k, axis=1, mode="promise_in_bounds")
                total = total + jnp.maximum(1.0 - jnp.abs(shifted - float(s)), 0.0) * got
            return total

        total = lax.fori_loop(0, count, tiles, jnp.zeros((8, 128), F32))
        acc[:, cols] = acc[:, cols] + weight * total
        return carry

    lax.fori_loop(0, most, task, 0)
    out_ref[...] = acc[0:4, :] + acc[4:8, :]


def geometry(first_row, rows_dev):
    rows = first_row + jnp.arange(rows_dev, dtype=jnp.int32)
    yy = ((rows.astype(F32) + 0.5) / NPIX * 2.0 - 1.0)[:, None]
    xx = ((jnp.arange(NPIX, dtype=jnp.int32).astype(F32) + 0.5) / NPIX * 2.0 - 1.0)[None, :]
    dist = jnp.sqrt(xx * xx + yy * yy)
    upos = (dist - R_INNER) / (1.0 - R_INNER) * NR - 0.5
    vpos = (jnp.arctan2(yy, xx) + jnp.pi) / (2.0 * jnp.pi) * NPHI - 0.5
    return jnp.concatenate([upos, upos], axis=0), jnp.concatenate([vpos, vpos], axis=0)


def body(density, velocity, shifts, fractions):
    phi, row = lax.axis_index("phi"), lax.axis_index("row")
    sds = lambda *s: jax.ShapeDtypeStruct(s, F32)
    dma = lambda *s: pltpu.SemaphoreType.DMA(s)
    vmem = lambda *s: pltpu.VMEM(s, F32)
    cyc = pl.pallas_call(
        first_kernel, name="first", out_shape=sds(64, 4, 8, 128),
        in_specs=[VM, VM], out_specs=ANY,
        scratch_shapes=[
            vmem(4, 4, 144, 128), vmem(2, 16, 128), vmem(2, 4, 32, 128), vmem(2, 16, 128), vmem(2, 128, 128),
            vmem(64, 4, 8, 128), dma(6), dma(6), dma(64), dma(64), pltpu.SemaphoreType.DMA,
        ],
        compiler_params=pltpu.CompilerParams(collective_id=0, has_side_effects=True),
    )(density, velocity)
    back, table, rho_back = pl.pallas_call(
        second_kernel, name="second", out_shape=(sds(64, 3, 8, 128), sds(4, 34, 16, 128), sds(64, 8, 128)),
        in_specs=[SM, SM, VM], out_specs=(ANY, ANY, VM),
        scratch_shapes=[
            vmem(64, 4, 8, 128), vmem(2, 8, 4, 8, 128), vmem(2, 64, 4, 128), vmem(2, 8, 4, 8, 128), vmem(2, 64, 4, 128),
            vmem(64, 4, 8, 128), vmem(512, 128), vmem(16, 128),
            dma(4), dma(4), dma(64), dma(64), dma(64), dma(64), dma(3), dma(8), dma(8),
            dma(16, 4), dma(16, 4), dma(16, 4), dma(16, 4), dma(32), dma(32),
        ],
        compiler_params=pltpu.CompilerParams(collective_id=1, has_side_effects=True),
    )(shifts, fractions, cyc)
    plan = sample_plan(4)
    most = plan.shape[1]
    words = plan[..., 0] + 8 * plan[..., 1] + 32 * (plan[..., 2] + 1) + 8192 * plan[..., 3]
    upos, vpos = geometry((phi * 4 + row) * 4, 4)
    return pl.pallas_call(
        functools.partial(last_kernel, most=most), name="last",
        out_shape=(sds(16, 32, 128), sds(3, 16, 32, 128), sds(4, 1024)),
        in_specs=[SM, VM, VM, VM, VM, VM], out_specs=(VM, VM, VM),
        scratch_shapes=[pltpu.VMEM((8, 1024), F32)],
    )(jnp.asarray(words.reshape(-1)), upos, vpos, rho_back, back, table.reshape(4, 544, 128))


def solution(mesh):
    in_specs = (P("phi", None, "row"), P(None, "phi", None, "row"), P("row"), P("row"))
    out_specs = (P("phi", None, "row"), P(None, "phi", None, "row"), P(("phi", "row"), None))
    return jax.shard_map(body, mesh=mesh, in_specs=in_specs, out_specs=out_specs, check_vma=False)
```

time: 174 us -> 120 us (0.69)
  Pallas kernels: 163 us -> 118 us
  local copies, waits for them, and re-layouts: 4.46 us -> 0 us
  between operations: 3.37 us -> 0.67 us
    pallas_call x11 -> x3, Pallas kernels: 163 us -> 118 us  [the longest x1 64.9 us: body(): pl.pallas_call(second_kernel, name='second', out_shape=(sds(64, 3, 8, 128...]
    dynamic_slice x2 -> x0, local copies, waits for them, and re-layouts: 2.47 us -> none  [the longest x1 1.24 us: body(): shift = lax.dynamic_index_in_dim(shifts, local, keepdims=False)]
where the time goes in v2:
time: 120 us
  Pallas kernels  118 us (98%)
  other arithmetic  1.45 us (1%)
    pallas_call x1, Pallas kernels, body(): pl.pallas_call(second_kernel, name='second', out_shape=(sds(64, 3, 8, 128...  64.9 us
    pallas_call x1, Pallas kernels, body(): pl.pallas_call(first_kernel, name='first', out_shape=sds(64, 4, 8, 128),...  43.5 us
    pallas_call x1, Pallas kernels, body(): pl.pallas_call(functools.partial(last_kernel, most=most), name='last', ou...  9.35 us

profile of v2, /device:TPU:77, one launch (start us, length us, event | category | flops | bytes accessed | tf_op | source)
XLA Modules:
  0.0 119.8 jit_solution(16778965984421458553)
XLA Ops:
  0.7 0.1 multiply_add_fusion
  0.8 0.1 multiply_add_fusion.1
  0.9 0.6 pad_maximum_fusion.u_ref
  1.5 0.6 pad_maximum_fusion.1.v_ref
  2.1 43.5 %first.1.cyc = f32[64,4,8,128]{3,2,1,0:T(8,128)} custom-call(f32[16,32,128]{2,1,0:T(8,128)} %rho_ref.1, f32[3,16,32,128]{3,2,1,0:T(8,128)} %vel_ref.1), custom_call_target="tpu_custom_call" | custom-call | tf_op jit(solution)/shard_map/first/pallas_call | solution.py:594
  45.6 64.9 %second.1 = (f32[64,3,8,128]{3,2,1,0:T(8,128)}, f32[4,34,16,128]{3,2,1,0:T(8,128)}, f32[64,8,128]{2,1,0:T(8,128)}) custom-call(s32[16]{0:T(128)} %shift_ref.1, f32[16]{0:T(128)} %frac_ref.1, f32[64,4,8,128]{3,2,1,0:T(8,128)} %first.1.cyc), custom_call_target="tpu_custom_call" | custom-call | tf_op jit(solution)/shard_map/second/pallas_call | solution.py:603
  110.4 9.4 %last.1 = (f32[16,32,128]{2,1,0:T(8,128)}, f32[3,16,32,128]{3,2,1,0:T(8,128)}, f32[4,1024]{1,0:T(4,128)}) custom-call(s32[4096]{0:T(1024)} %constant.49.clone.plan_ref, f32[8,1024]{1,0:T(8,128)} %pad_maximum_fusion.u_ref, f32[8,1024]{1,0:T(8,128)} %pad_maximum_fusion.1.v_ref, f32[64,8,128]{2,1,0:T(8,128)} %get-tuple-element.6.rho_src, ...), custom_call_target="tpu_custom_call" | custom-call | tf_op jit(solution)/shard_map/last/pallas_call | solution.py:618
  (3 shorter events, 0.0 us)

commit v3 on v2

v3 whole, which is shorter than its diff:
```python
import functools

import jax
import jax.numpy as jnp
import numpy as np
from jax import lax
from jax.experimental import pallas as pl
from jax.experimental.pallas import tpu as pltpu
from jax.sharding import PartitionSpec as P

MESH = pl.DeviceIdType.MESH
BAND = 8
NPIX = 1024
NPHI = 1024
NR = 512
NTH = 32
UNROLL = 4
KAPPA = 1.5
R_INNER = 0.2
F32 = jnp.float32
VM = pl.BlockSpec(memory_space=pltpu.VMEM)
SM = pl.BlockSpec(memory_space=pltpu.SMEM)
ANY = pl.BlockSpec(memory_space=pl.ANY)


def where_of(band, group):
    return (band % 8) * 8 + group * 2 + band // 8


def lanes():
    return lax.broadcasted_iota(jnp.int32, (8, 128), 1)


def conserved(q):
    return [q[0], q[0] * q[1], q[0] * q[2], q[0] * q[3]]


def side(q, comp, offset):
    m = q[0] * (0.5 * q[comp] + offset)
    out = [m, m * q[1], m * q[2], m * q[3]]
    out[comp] = out[comp] + 0.5 * q[0]
    return out


def updated(here, lower, upper):
    total = None
    for (comp, low), (_, high) in zip(lower, upper):
        p, m = side(low, comp, 0.75), side(high, comp, -0.75)
        part = [b - a for a, b in zip(p, m)]
        total = part if total is None else [s + t for s, t in zip(total, part)]
    new = [0.775 * c - 0.05 * t for c, t in zip(conserved(here), total)]
    inv = 1.0 / new[0]
    return [new[0], new[1] * inv, new[2] * inv, new[3] * inv]


def spread(i):
    return jnp.where(i % 2 == 0, 4 + i // 2, 4 - (i + 1) // 2)


def signal(peer):
    pl.semaphore_signal(pltpu.get_barrier_semaphore(), inc=1, device_id=peer, device_id_type=MESH)


def remote(src, dst, ssem, rsem, to):
    return pltpu.make_async_remote_copy(src, dst, ssem, rsem, device_id=to, device_id_type=MESH)


def wait_all(ref, sems):
    for sem in sems:
        pltpu.make_async_copy(ref, ref, sem).wait()


def main_kernel(
    shift_ref, frac_ref, rho_ref, vel_ref, back, table, rho_back, u_ref, v_ref,
    pad, edge, hphi, hr, ht, stepped, cyc, t1, th_edge, r_edge, hth, hr2, fin, flat, light,
    es, er, as_, ar, bs, br, rs, rr, vs, vr, ls, us, ur, hs, hrr, ps, pr, gs, gr,
):
    phi, row = lax.axis_index("phi"), lax.axis_index("row")
    z, x, y = phi // 8, lax.rem(phi // 2, 4), lax.rem(phi, 2)
    half, zl, xy = z // 4, lax.rem(z, 4), lax.rem(phi, 8)
    core, yh = lax.rem(row, 2), row // 2
    band = row * 16 + y * 8 + z

    def at_band(b):
        j = lax.rem(b, 16)
        return {"phi": lax.rem(j, 8) * 8 + x * 2 + j // 8, "row": b // 16}

    def at_group(g):
        return {"phi": z * 8 + g * 2 + y}

    def chip(n):
        m = lax.rem(xy * 2 + yh + n, 16)
        return {"phi": z * 8 + m // 2, "row": lax.rem(m, 2) * 2 + core}

    sibling = {"row": yh * 2 + 1 - core}
    phi_low, phi_high = {"phi": lax.rem(phi + 63, 64)}, {"phi": lax.rem(phi + 1, 64)}
    row_low, row_high = {"row": lax.rem(row + 3, 4)}, {"row": lax.rem(row + 1, 4)}
    band_low, band_high = at_band(lax.rem(band + 63, 64)), at_band(lax.rem(band + 1, 64))
    group_low, group_high = at_group(lax.rem(x + 3, 4)), at_group(lax.rem(x + 1, 4))

    def greet_phi(d, c):
        signal({"phi": lax.rem(phi + d, 64)})
        return c

    def greet_chip(n, c):
        signal(chip(n))
        return c

    lax.fori_loop(1, 64, greet_phi, 0)
    for peer in (row_low, row_high, band_low, band_high, sibling):
        signal(peer)
    lax.fori_loop(1, 16, greet_chip, 0)

    for f in range(4):
        for g in range(4):
            src = rho_ref[:, 8 * g : 8 * g + 8, :] if f == 0 else vel_ref[f - 1, :, 8 * g : 8 * g + 8, :]
            t = src.reshape(128, 128).T
            pad[f, g, 8:136, :] = t
            edge[0, pl.ds(f * 4 + g, 1), :] = t[0:1, :]
            edge[1, pl.ds(f * 4 + g, 1), :] = t[127:128, :]
    pl.semaphore_wait(pltpu.get_barrier_semaphore(), 83)
    copies = [
        remote(rho_ref.at[15], hphi.at[0, 0], es.at[0], er.at[0], phi_high),
        remote(vel_ref.at[:, 15], hphi.at[0, pl.ds(1, 3)], es.at[1], er.at[1], phi_high),
        remote(rho_ref.at[0], hphi.at[1, 0], es.at[2], er.at[2], phi_low),
        remote(vel_ref.at[:, 0], hphi.at[1, pl.ds(1, 3)], es.at[3], er.at[3], phi_low),
        remote(edge.at[1], hr.at[0], es.at[4], er.at[4], row_high),
        remote(edge.at[0], hr.at[1], es.at[5], er.at[5], row_low),
    ]
    for c in copies:
        c.start()
    for c in copies:
        c.wait()
    has_low = jnp.where(row > 0, 1.0, 0.0)
    has_high = jnp.where(row < 3, 1.0, 0.0)
    for pair in range(2):
        ht[pair] = jnp.concatenate([hphi[s, 2 * pair + f] for f in range(2) for s in range(2)], axis=0).T
    for f in range(4):
        for g in range(4):
            pad[f, g, 7:8, :] = hr[0, pl.ds(f * 4 + g, 1), :] * has_low
            pad[f, g, 136:137, :] = hr[1, pl.ds(f * 4 + g, 1), :] * has_high

    lane = lanes()
    lane8 = lane % 8
    first, last = lane < 8, lane >= 120
    low_th, high_th = lane8 == 0, lane8 == 7
    zero = jnp.zeros((8, 128), F32)

    def band_at(i):
        return lax.rem(z + spread(i // 2), 8) + 8 * (i % 2)

    def spot(i, g):
        j = band_at(i)
        return lax.rem(j, 8) * 8 + g * 2 + j // 8

    own = pltpu.make_async_copy(stepped.at[phi], cyc.at[phi], ls.at[0])

    def send_tiles(i):
        for g in range(4):
            d = spot(i, g)

            @pl.when(d != phi)
            def _():
                remote(stepped.at[d], cyc.at[phi], as_, ar, {"phi": d}).start()

            @pl.when(d == phi)
            def _():
                own.start()

    def step(i, carry):
        base = pl.multiple_of(8 * band_at(i), 8)
        here = [[pad[f, g, pl.ds(base + 8, 8), :] for f in range(4)] for g in range(4)]
        side_edge = [ht[pair, pl.ds(base, 8), :] for pair in range(2)]
        for g in range(4):
            c = here[g]
            before = [pad[f, g, pl.ds(base, 16), :][7:15] for f in range(4)]
            after = [pad[f, g, pl.ds(base + 8, 16), :][1:9] for f in range(4)]
            thm, thp, phm, php = [], [], [], []
            for f in range(4):
                lo = pltpu.roll(here[g - 1][f], 121, 1) if g > 0 else zero
                hi = pltpu.roll(here[g + 1][f], 7, 1) if g < 3 else zero
                thm.append(jnp.where(low_th, lo, pltpu.roll(c[f], 1, 1)))
                thp.append(jnp.where(high_th, hi, pltpu.roll(c[f], 127, 1)))
                off = (f % 2) * 64 + g * 8
                lo = pltpu.roll(side_edge[f // 2], (128 - off) % 128, 1)
                hi = pltpu.roll(side_edge[f // 2], (120 - off - 32) % 128, 1)
                phm.append(jnp.where(first, lo, pltpu.roll(c[f], 8, 1)))
                php.append(jnp.where(last, hi, pltpu.roll(c[f], 120, 1)))
            new = updated(c, ((2, phm), (3, thm), (1, before)), ((2, php), (3, thp), (1, after)))
            d = spot(i, g)
            for f in range(4):
                stepped[d, f] = new[f]

        @pl.when(i > 0)
        def _():
            send_tiles(i - 1)

        return carry

    lax.fori_loop(0, 16, step, 0)
    send_tiles(15)

    local = z + 8 * y
    shift = shift_ref[local]
    w = frac_ref[local]
    whole, remain = shift // 16, shift % 16
    one, two = 8 * remain, 8 * (remain + 1)
    two_roll = lax.rem(two, 128)
    keep_one, keep_two = lane >= one, lane >= two

    def turn(tiles):
        return [pltpu.roll(t, one, 1) for t in tiles] + [pltpu.roll(t, two_roll, 1) for t in tiles]

    def blend(cur, prev):
        out = []
        for f in range(4):
            lead = jnp.where(keep_one, cur[f], prev[f])
            trail = jnp.where(keep_two, cur[4 + f], prev[4 + f])
            out.append((1.0 - w) * lead + w * trail)
        return out

    def cycle_slab(p):
        slab = lax.rem(p + 128 - whole, 64)
        return turn([cyc[slab, f] for f in range(4)])

    def move(big, prev):
        top, bottom = [None] * 4, [None] * 4
        for j in range(8):
            cur = cycle_slab(big * 8 + j)
            out = blend(cur, prev)
            prev = cur
            for f in range(4):
                t = out[f]
                t1[big * 8 + j, f] = t
                hi = pltpu.roll(t, (j - 7) % 128, 1)
                lo = pltpu.roll(t, j, 1)
                top[f] = hi if j == 0 else jnp.where(lane8 == j, hi, top[f])
                bottom[f] = lo if j == 0 else jnp.where(lane8 == j, lo, bottom[f])
                r_edge[0, big * 8 + j, pl.ds(f, 1), :] = t[0:1, :]
                r_edge[1, big * 8 + j, pl.ds(f, 1), :] = t[7:8, :]
        for f in range(4):
            th_edge[0, big, f] = bottom[f]
            th_edge[1, big, f] = top[f]
        return prev

    pixel = (phi * 4 + row) * 4 + lax.broadcasted_iota(jnp.int32, (8, 1024), 0) % 4
    column = lax.broadcasted_iota(jnp.int32, (8, 1024), 1)
    yy = (pixel.astype(F32) + 0.5) / NPIX * 2.0 - 1.0
    xx = (column.astype(F32) + 0.5) / NPIX * 2.0 - 1.0
    dist = jnp.sqrt(xx * xx + yy * yy)
    u_ref[...] = (dist - R_INNER) / (1.0 - R_INNER) * NR - 0.5
    v_ref[...] = (jnp.arctan2(yy, xx) + jnp.pi) / (2.0 * jnp.pi) * NPHI - 0.5

    wait_all(cyc.at[pl.ds(0, 63)], (as_, ar))
    own.wait()
    lax.fori_loop(0, 8, move, cycle_slab(-1))
    copies = [
        remote(r_edge.at[1], hr2.at[0], bs.at[0], br.at[0], band_high),
        remote(r_edge.at[0], hr2.at[1], bs.at[1], br.at[1], band_low),
        remote(th_edge.at[1], hth.at[0], bs.at[2], br.at[2], group_high),
        remote(th_edge.at[0], hth.at[1], bs.at[3], br.at[3], group_low),
    ]
    for c in copies:
        c.start()
    for c in copies:
        c.wait()
    for side_of, cond in enumerate((band > 0, band < 63)):
        hr2[side_of] = hr2[side_of] * jnp.where(cond, 1.0, 0.0)
    for side_of, cond in enumerate((x > 0, x < 3)):
        hth[side_of] = hth[side_of] * jnp.where(cond, 1.0, 0.0)

    sub = lax.broadcasted_iota(jnp.int32, (8, 128), 0)
    low_r, high_r = sub == 0, sub == 7

    def hydro_slab(p):
        q = lax.rem(p + 128 - whole, 64)
        before, after = lax.rem(q + 63, 64), lax.rem(q + 1, 64)
        big, j = q // 8, lax.rem(q, 8)
        back_by = lax.rem(128 - j, 128)
        c = [t1[q, f] for f in range(4)]
        thm, thp, phm, php, rm, rp = [], [], [], [], [], []
        for f in range(4):
            thm.append(jnp.where(low_th, pltpu.roll(hth[0, big, f], back_by, 1), pltpu.roll(c[f], 1, 1)))
            thp.append(jnp.where(high_th, pltpu.roll(hth[1, big, f], 7 - j, 1), pltpu.roll(c[f], 127, 1)))
            phm.append(jnp.where(first, pltpu.roll(t1[before, f], 8, 1), pltpu.roll(c[f], 8, 1)))
            php.append(jnp.where(last, pltpu.roll(t1[after, f], 120, 1), pltpu.roll(c[f], 120, 1)))
            lo = jnp.broadcast_to(hr2[0, q, pl.ds(f, 1), :], (8, 128))
            hi = jnp.broadcast_to(hr2[1, q, pl.ds(f, 1), :], (8, 128))
            rm.append(jnp.where(low_r, lo, pltpu.roll(c[f], 1, 0)))
            rp.append(jnp.where(high_r, hi, pltpu.roll(c[f], 7, 0)))
        new = updated(c, ((2, phm), (3, thm), (1, rm)), ((2, php), (3, thp), (1, rp)))
        return turn(new)

    def rho_message(p):
        return remote(fin.at[p, 0], rho_back.at[phi], rs, rr, {"phi": p})

    def vel_message(p):
        return remote(fin.at[p, pl.ds(1, 3)], back.at[phi], vs, vr, {"phi": p})

    own_rho = pltpu.make_async_copy(fin.at[phi, 0], rho_back.at[phi], ls.at[1])
    own_vel = pltpu.make_async_copy(fin.at[phi, pl.ds(1, 3)], back.at[phi], ls.at[2])

    def send(zoff, message, own_message):
        def one_slab(i, c):
            p = lax.rem(z + zoff, 8) * 8 + i

            @pl.when(p != phi)
            def _():
                message(p).start()

            @pl.when(p == phi)
            def _():
                own_message.start()

            return c

        lax.fori_loop(0, 8, one_slab, 0)

    def block(i, carry):
        start = lax.rem(z + spread(i), 8) * 8

        def slab(k, prev):
            cur = hydro_slab(start + k)
            out = blend(cur, prev)
            for f in range(4):
                fin[start + k, f] = out[f]
            return cur

        lax.fori_loop(0, 8, slab, hydro_slab(start - 1), unroll=UNROLL)

        @pl.when(i > 0)
        def _():
            send(spread(i - 1), rho_message, own_rho)

        @pl.when(i == 5)
        def _():
            send(4, vel_message, own_vel)

        return carry

    lax.fori_loop(0, 8, block, 0)
    send(0, rho_message, own_rho)
    for off in (1, 7, 0):
        send(off, vel_message, own_vel)

    wait_all(rho_back.at[pl.ds(0, 63)], (rs, rr))
    own_rho.wait()
    for g in range(4):
        t = jnp.concatenate([rho_back[where_of(j, g)] for j in range(16)], axis=0).T.reshape(16, 8, 128)
        for i in range(16):
            flat[pl.ds(i * 32 + 8 * g, 8), :] = t[i]
    k = row * 128 + lax.broadcasted_iota(jnp.int32, (16, 128), 1)
    radius = R_INNER + (k.astype(F32) + 0.5) * (1.0 - R_INNER) / NR
    seen = jnp.ones((16, 128), F32)
    total = jnp.zeros((16, 128), F32)
    for j in range(NTH):
        tilt = float(np.float32(1.0 + 0.5 * np.cos(np.pi * (j + 0.5) / NTH)))
        t = jnp.exp(flat[pl.ds(j, 16, stride=32), :] * (-KAPPA / NTH))
        total = total + tilt * ((1.0 - t) * seen)
        seen = seen * t
    light[...] = (1.0 / jnp.sqrt(radius)) * total

    own_light = pltpu.make_async_copy(light, table.at[row, xy, zl], ls.at[3])
    own_light.start()

    def up(n):
        to = {"phi": (half * 4 + lax.rem(zl + n, 4)) * 8 + xy}
        return remote(light, table.at[row, xy, zl], us.at[n], ur.at[n], to)

    def over(n, end):
        to = {"phi": ((1 - half) * 4 + lax.rem(zl + n, 4)) * 8 + xy}
        return remote(light, table.at[row, 8, end], us.at[4 + n], ur.at[4 + n], to)

    ends = ((1, 0, 0), (0, 7, 3))
    for n in (2, 1, 3):
        up(n).start()
    for end, at, plane in ends:

        @pl.when((xy == at) & (zl == plane))
        def _(end=end):
            for n in range(4):
                over(n, end).start()

    for off in (3, 5, 2, 6):
        send(off, vel_message, own_vel)
    for n in (1, 2, 3):
        up(n).wait()
    own_light.wait()
    for end, at, plane in ends:

        @pl.when((xy == at) & (zl == plane))
        def _(end=end):
            for n in range(4):
                over(n, end).wait_send()

        for pos in range(4):

            @pl.when((xy == at) & (zl == pos))
            def _(end=end, pos=pos, plane=plane):
                over((pos - plane) % 4, end).wait_recv()

    def part(q, pos, ssem, rsem, to):
        return remote(table.at[q, pos], table.at[q, pos], ssem, rsem, to)

    def outer(q, end, ssem, rsem, to):
        return remote(table.at[q, 8, end], table.at[q, 8, end], ssem, rsem, to)

    def to_chip(n, c):
        part(row, xy, ps.at[n], pr.at[n], chip(n)).start()
        for end, at, _ in ends:

            @pl.when(xy == at)
            def _(end=end):
                outer(row, end, hs.at[n], hrr.at[n], chip(n)).start()

        return c

    def give(q, pos, n):
        part(q, pos, gs.at[n], gr.at[n], sibling).start()
        for end, at, _ in ends:

            @pl.when(pos == at)
            def _(end=end):
                outer(q, end, hs.at[16 + n], hrr.at[16 + n], sibling).start()

    def source(n):
        m = lax.rem(xy * 2 + yh + 16 - n, 16)
        return m // 2, lax.rem(m, 2)

    def from_chip(n, c):
        pos, high = source(n)
        q = high * 2 + core
        part(q, pos, ps.at[n], pr.at[n], chip(n)).wait_recv()
        for end, at, _ in ends:

            @pl.when(pos == at)
            def _(end=end):
                outer(q, end, hs.at[n], hrr.at[n], chip(n)).wait_recv()

        give(q, pos, n)
        return c

    def finish(n, c):
        pos, high = source(n)
        q, other = high * 2 + core, high * 2 + 1 - core
        part(q, pos, gs.at[n], gr.at[n], sibling).wait_send()
        part(other, pos, gs.at[n], gr.at[n], sibling).wait_recv()
        for end, at, _ in ends:

            @pl.when(pos == at)
            def _(end=end):
                outer(q, end, hs.at[16 + n], hrr.at[16 + n], sibling).wait_send()
                outer(other, end, hs.at[16 + n], hrr.at[16 + n], sibling).wait_recv()

        return c

    def sent(n, c):
        part(row, xy, ps.at[n], pr.at[n], chip(n)).wait_send()
        for end, at, _ in ends:

            @pl.when(xy == at)
            def _(end=end):
                outer(row, end, hs.at[n], hrr.at[n], chip(n)).wait_send()

        return c

    lax.fori_loop(1, 16, to_chip, 0)
    give(row, xy, 0)
    lax.fori_loop(1, 16, from_chip, 0)
    lax.fori_loop(0, 16, finish, 0)
    lax.fori_loop(1, 16, sent, 0)
    wait_all(back.at[pl.ds(0, 63)], (vs, vr))
    own_vel.wait()


@functools.lru_cache(maxsize=None)
def sample_plan(rows_dev):
    yy = ((np.arange(NPIX) + 0.5) / NPIX * 2.0 - 1.0)[:, None]
    xx = ((np.arange(NPIX) + 0.5) / NPIX * 2.0 - 1.0)[None, :]
    u = (np.sqrt(xx * xx + yy * yy) - R_INNER) / (1.0 - R_INNER) * NR - 0.5
    v = (np.arctan2(yy, xx) + np.pi) / (2.0 * np.pi) * NPHI - 0.5
    blocks = NPIX // rows_dev
    plans = []
    for b in range(blocks):
        plan = []
        for c in range(NPIX // 128):
            cut = np.s_[b * rows_dev : (b + 1) * rows_dev, c * 128 : (c + 1) * 128]
            uu, vv = u[cut], v[cut]
            for q in range(NR // 128):
                hit = (uu > q * 128 - 1.01) & (uu < q * 128 + 128.01)
                if hit.any():
                    lo = int(np.floor((vv[hit].min() - 0.01) / 8))
                    hi = int(np.floor((np.floor(vv[hit].max() + 0.01) + 1) / 8))
                    plan.append((c, q, lo, hi - lo + 1))
        plans.append(plan)
    most = max(len(p) for p in plans)
    table = np.zeros((blocks, most, 4), np.int32)
    for b, plan in enumerate(plans):
        table[b, : len(plan)] = plan
    return table


def last_kernel(plan_ref, u_ref, v_ref, rho_src, vel_src, w_ref, rho_ref, vel_ref, out_ref, acc, *, most):
    phi, row = lax.axis_index("phi"), lax.axis_index("row")
    for f in range(4):
        for g in range(4):
            x = jnp.concatenate(
                [rho_src[where_of(j, g)] if f == 0 else vel_src[where_of(j, g), f - 1] for j in range(16)], axis=0
            )
            t = x.T.reshape(16, 8, 128)
            if f == 0:
                rho_ref[:, 8 * g : 8 * g + 8, :] = t
            else:
                vel_ref[f - 1, :, 8 * g : 8 * g + 8, :] = t
    spot = phi * 4 + row
    first_tile = phi // 32 * 64
    acc[...] = jnp.zeros_like(acc)
    sub = lax.broadcasted_iota(jnp.int32, (8, 128), 0)

    def task(t, carry):
        word = plan_ref[spot * most + t]
        chunk, q = word % 8, word // 8 % 4
        lo, count = word // 32 % 256 - 1, word // 8192
        cols = pl.ds(pl.multiple_of(chunk * 128, 128), 128)
        u, v = u_ref[:, cols], v_ref[:, cols]
        floor = jnp.floor(u)
        part = u - floor
        k = floor.astype(jnp.int32) - q * 128 + jnp.where(sub >= 4, 1, 0)
        weight = jnp.where(sub >= 4, part, 1.0 - part)
        weight = jnp.where((k >= 0) & (k < 128), weight, 0.0)
        k = jnp.clip(k, 0, 127)

        def tiles(i, total):
            base = (lo + i) * 8
            near = lo + i - first_tile
            slab = jnp.where(near < 0, 32, jnp.where(near > 63, 33, near // 2 % 8 * 4 + near // 16))
            start = pl.multiple_of(slab * 16 + (near + 2) % 2 * 8, 8)
            block = w_ref[q, pl.ds(start, 8), :]
            shifted = v - base.astype(F32)
            for s in range(8):
                line = jnp.broadcast_to(block[s : s + 1, :], (8, 128))
                got = jnp.take_along_axis(line, k, axis=1, mode="promise_in_bounds")
                total = total + jnp.maximum(1.0 - jnp.abs(shifted - float(s)), 0.0) * got
            return total

        total = lax.fori_loop(0, count, tiles, jnp.zeros((8, 128), F32))
        acc[:, cols] = acc[:, cols] + weight * total
        return carry

    lax.fori_loop(0, most, task, 0)
    out_ref[...] = acc[0:4, :] + acc[4:8, :]


def body(density, velocity, shifts, fractions):
    sds = lambda *s: jax.ShapeDtypeStruct(s, F32)
    dma = lambda *s: pltpu.SemaphoreType.DMA(s)
    vmem = lambda *s: pltpu.VMEM(s, F32)
    one = pltpu.SemaphoreType.DMA
    back, table, rho_back, upos, vpos = pl.pallas_call(
        main_kernel, name="main", out_shape=(sds(64, 3, 8, 128), sds(4, 9, 4, 16, 128), sds(64, 8, 128), sds(8, 1024), sds(8, 1024)),
        in_specs=[SM, SM, VM, VM], out_specs=(ANY, ANY, VM, VM, VM),
        scratch_shapes=[
            vmem(4, 4, 144, 128), vmem(2, 16, 128), vmem(2, 4, 32, 128), vmem(2, 16, 128), vmem(2, 128, 128),
            vmem(64, 4, 8, 128), vmem(64, 4, 8, 128), vmem(64, 4, 8, 128),
            vmem(2, 8, 4, 8, 128), vmem(2, 64, 4, 128), vmem(2, 8, 4, 8, 128), vmem(2, 64, 4, 128),
            vmem(64, 4, 8, 128), vmem(512, 128), vmem(16, 128),
            dma(6), dma(6), one, one, dma(4), dma(4), one, one, one, one, dma(4), dma(8), dma(8),
            dma(32), dma(32), dma(16), dma(16), dma(16), dma(16),
        ],
        compiler_params=pltpu.CompilerParams(collective_id=0, has_side_effects=True),
    )(shifts, fractions, density, velocity)
    plan = sample_plan(4)
    most = plan.shape[1]
    words = plan[..., 0] + 8 * plan[..., 1] + 32 * (plan[..., 2] + 1) + 8192 * plan[..., 3]
    return pl.pallas_call(
        functools.partial(last_kernel, most=most), name="last",
        out_shape=(sds(16, 32, 128), sds(3, 16, 32, 128), sds(4, 1024)),
        in_specs=[SM, VM, VM, VM, VM, VM], out_specs=(VM, VM, VM),
        scratch_shapes=[pltpu.VMEM((8, 1024), F32)],
    )(jnp.asarray(words.reshape(-1)), upos, vpos, rho_back, back, table.reshape(4, 576, 128))


def solution(mesh):
    in_specs = (P("phi", None, "row"), P(None, "phi", None, "row"), P("row"), P("row"))
    out_specs = (P("phi", None, "row"), P(None, "phi", None, "row"), P(("phi", "row"), None))
    return jax.shard_map(body, mesh=mesh, in_specs=in_specs, out_specs=out_specs, check_vma=False)
```

time: 120 us -> 97.3 us (0.81)
  Pallas kernels: 118 us -> 95.9 us
  other arithmetic: 1.45 us -> 0 us
    pallas_call x2 -> x1, Pallas kernels: 108 us -> 86.3 us  [body(): pl.pallas_call(main_kernel, name='main', out_shape=(sds(64, 3, 8, 128), s...]
    concatenate x2 -> x0, other arithmetic: 1.22 us -> none  [the longest x1 0.61 us: geometry(): jnp.concatenate([upos, upos], axis=0)]
where the time goes in v3:
time: 97.3 us; the launch traced here: 96.5 us
  Pallas kernels  95.9 us (99%)
    pallas_call x1, Pallas kernels, body(): pl.pallas_call(main_kernel, name='main', out_shape=(sds(64, 3, 8, 128), s...  86.3 us
    pallas_call x1, Pallas kernels, body(): pl.pallas_call(functools.partial(last_kernel, most=most), name='last', ou...  9.58 us

profile of v3, /device:TPU:77, one launch (start us, length us, event | category | flops | bytes accessed | tf_op | source)
XLA Modules:
  0.0 96.5 jit_solution(17157181304339625692)
XLA Ops:
  0.6 86.3 %main.1 = (f32[64,3,8,128]{3,2,1,0:T(8,128)}, f32[4,9,4,16,128]{4,3,2,1,0:T(8,128)}, f32[64,8,128]{2,1,0:T(8,128)}, f32[8,1024]{1,0:T(8,128)}, f32[8,1024]{1,0:T(8,128)}) custom-call(s32[16]{0:T(128)} %shift_ref.1, f32[16]{0:T(128)} %frac_ref.1, f32[16,32,128]{2,1,0:T(8,128)} %rho_ref.1, f32[3,16,32,128]{3,2,1,0:T(8,128)} %vel_ref.1), custom_call_target="tpu_custom_call" | custom-call | tf_op jit(solution)/shard_map/main/pallas_call | solution.py:559
  86.9 9.6 %last.1 = (f32[16,32,128]{2,1,0:T(8,128)}, f32[3,16,32,128]{3,2,1,0:T(8,128)}, f32[4,1024]{1,0:T(4,128)}) custom-call(s32[4096]{0:T(1024)} %constant.2.clone.plan_ref, f32[8,1024]{1,0:T(8,128)} %get-tuple-element.8.u_ref, f32[8,1024]{1,0:T(8,128)} %get-tuple-element.9.v_ref, f32[64,8,128]{2,1,0:T(8,128)} %get-tuple-element.10.rho_src, ...), custom_call_target="tpu_custom_call" | custom-call | tf_op jit(solution)/shard_map/last/pallas_call | solution.py:575

commit v4 on v3

--- a/solution.py
+++ b/solution.py
@@ -31,6 +31,10 @@
     return lax.broadcasted_iota(jnp.int32, (8, 128), 1)
 
 
+def rolled(tiles, by, axis=1):
+    return [pltpu.roll(t, by, axis) for t in tiles]
+
+
 def conserved(q):
     return [q[0], q[0] * q[1], q[0] * q[2], q[0] * q[3]]
 
@@ -71,8 +75,8 @@
 
 
 def main_kernel(
-    shift_ref, frac_ref, rho_ref, vel_ref, back, table, rho_back, u_ref, v_ref,
-    pad, edge, hphi, hr, ht, stepped, cyc, t1, th_edge, r_edge, hth, hr2, fin, flat, light,
+    shift_ref, frac_ref, rho_in, vel_in, back, table, rho_back, u_ref, v_ref,
+    rho_ref, vel_ref, pad, edge, hphi, hr, ht, stepped, cyc, t1, th_edge, r_edge, hth, hr2, fin, flat, light,
     es, er, as_, ar, bs, br, rs, rr, vs, vr, ls, us, ur, hs, hrr, ps, pr, gs, gr,
 ):
     phi, row = lax.axis_index("phi"), lax.axis_index("row")
@@ -98,19 +102,33 @@
     band_low, band_high = at_band(lax.rem(band + 63, 64)), at_band(lax.rem(band + 1, 64))
     group_low, group_high = at_group(lax.rem(x + 3, 4)), at_group(lax.rem(x + 1, 4))
 
-    def greet_phi(d, c):
-        signal({"phi": lax.rem(phi + d, 64)})
+    loads = [
+        pltpu.make_async_copy(rho_in, rho_ref, ls.at[4]),
+        pltpu.make_async_copy(vel_in, vel_ref, ls.at[5]),
+    ]
+    for c in loads:
+        c.start()
+
+    def greet_phi(i, c):
+        peer = lax.rem(z + spread(i // 8), 8) * 8 + lax.rem(i, 8)
+
+        @pl.when(peer != phi)
+        def _():
+            signal({"phi": peer})
+
         return c
 
     def greet_chip(n, c):
         signal(chip(n))
         return c
 
-    lax.fori_loop(1, 64, greet_phi, 0)
+    lax.fori_loop(0, 64, greet_phi, 0)
     for peer in (row_low, row_high, band_low, band_high, sibling):
         signal(peer)
     lax.fori_loop(1, 16, greet_chip, 0)
 
+    for c in loads:
+        c.wait()
     for f in range(4):
         for g in range(4):
             src = rho_ref[:, 8 * g : 8 * g + 8, :] if f == 0 else vel_ref[f - 1, :, 8 * g : 8 * g + 8, :]
@@ -175,17 +193,15 @@
             c = here[g]
             before = [pad[f, g, pl.ds(base, 16), :][7:15] for f in range(4)]
             after = [pad[f, g, pl.ds(base + 8, 16), :][1:9] for f in range(4)]
-            thm, thp, phm, php = [], [], [], []
-            for f in range(4):
-                lo = pltpu.roll(here[g - 1][f], 121, 1) if g > 0 else zero
-                hi = pltpu.roll(here[g + 1][f], 7, 1) if g < 3 else zero
-                thm.append(jnp.where(low_th, lo, pltpu.roll(c[f], 1, 1)))
-                thp.append(jnp.where(high_th, hi, pltpu.roll(c[f], 127, 1)))
-                off = (f % 2) * 64 + g * 8
-                lo = pltpu.roll(side_edge[f // 2], (128 - off) % 128, 1)
-                hi = pltpu.roll(side_edge[f // 2], (120 - off - 32) % 128, 1)
-                phm.append(jnp.where(first, lo, pltpu.roll(c[f], 8, 1)))
-                php.append(jnp.where(last, hi, pltpu.roll(c[f], 120, 1)))
+            below = [pltpu.roll(here[g - 1][f], 121, 1) if g > 0 else zero for f in range(4)]
+            above = [pltpu.roll(here[g + 1][f], 7, 1) if g < 3 else zero for f in range(4)]
+            thm = [jnp.where(low_th, lo, t) for lo, t in zip(below, rolled(c, 1))]
+            thp = [jnp.where(high_th, hi, t) for hi, t in zip(above, rolled(c, 127))]
+            offs = [(f % 2) * 64 + g * 8 for f in range(4)]
+            below = [pltpu.roll(side_edge[f // 2], (128 - offs[f]) % 128, 1) for f in range(4)]
+            above = [pltpu.roll(side_edge[f // 2], (120 - offs[f] - 32) % 128, 1) for f in range(4)]
+            phm = [jnp.where(first, lo, t) for lo, t in zip(below, rolled(c, 8))]
+            php = [jnp.where(last, hi, t) for hi, t in zip(above, rolled(c, 120))]
             new = updated(c, ((2, phm), (3, thm), (1, before)), ((2, php), (3, thp), (1, after)))
             d = spot(i, g)
             for f in range(4):
@@ -209,7 +225,7 @@
     keep_one, keep_two = lane >= one, lane >= two
 
     def turn(tiles):
-        return [pltpu.roll(t, one, 1) for t in tiles] + [pltpu.roll(t, two_roll, 1) for t in tiles]
+        return rolled(tiles, one) + rolled(tiles, two_roll)
 
     def blend(cur, prev):
         out = []
@@ -229,13 +245,12 @@
             cur = cycle_slab(big * 8 + j)
             out = blend(cur, prev)
             prev = cur
+            hi, lo = rolled(out, (j - 7) % 128), rolled(out, j) if j else out
             for f in range(4):
                 t = out[f]
                 t1[big * 8 + j, f] = t
-                hi = pltpu.roll(t, (j - 7) % 128, 1)
-                lo = pltpu.roll(t, j, 1)
-                top[f] = hi if j == 0 else jnp.where(lane8 == j, hi, top[f])
-                bottom[f] = lo if j == 0 else jnp.where(lane8 == j, lo, bottom[f])
+                top[f] = hi[f] if j == 0 else jnp.where(lane8 == j, hi[f], top[f])
+                bottom[f] = lo[f] if j == 0 else jnp.where(lane8 == j, lo[f], bottom[f])
                 r_edge[0, big * 8 + j, pl.ds(f, 1), :] = t[0:1, :]
                 r_edge[1, big * 8 + j, pl.ds(f, 1), :] = t[7:8, :]
         for f in range(4):
@@ -272,24 +287,32 @@
     sub = lax.broadcasted_iota(jnp.int32, (8, 128), 0)
     low_r, high_r = sub == 0, sub == 7
 
-    def hydro_slab(p):
-        q = lax.rem(p + 128 - whole, 64)
-        before, after = lax.rem(q + 63, 64), lax.rem(q + 1, 64)
+    def at_slab(p):
+        return lax.rem(p + 192 - whole, 64)
+
+    def enter(p):
+        here = [t1[at_slab(p), f] for f in range(4)]
+        behind = rolled([t1[at_slab(p - 1), f] for f in range(4)], 8)
+        return here, behind, rolled(here, 120)
+
+    def hydro_slab(p, window):
+        c, phm_far, c_up = window
+        q = at_slab(p)
         big, j = q // 8, lax.rem(q, 8)
-        back_by = lax.rem(128 - j, 128)
-        c = [t1[q, f] for f in range(4)]
-        thm, thp, phm, php, rm, rp = [], [], [], [], [], []
-        for f in range(4):
-            thm.append(jnp.where(low_th, pltpu.roll(hth[0, big, f], back_by, 1), pltpu.roll(c[f], 1, 1)))
-            thp.append(jnp.where(high_th, pltpu.roll(hth[1, big, f], 7 - j, 1), pltpu.roll(c[f], 127, 1)))
-            phm.append(jnp.where(first, pltpu.roll(t1[before, f], 8, 1), pltpu.roll(c[f], 8, 1)))
-            php.append(jnp.where(last, pltpu.roll(t1[after, f], 120, 1), pltpu.roll(c[f], 120, 1)))
-            lo = jnp.broadcast_to(hr2[0, q, pl.ds(f, 1), :], (8, 128))
-            hi = jnp.broadcast_to(hr2[1, q, pl.ds(f, 1), :], (8, 128))
-            rm.append(jnp.where(low_r, lo, pltpu.roll(c[f], 1, 0)))
-            rp.append(jnp.where(high_r, hi, pltpu.roll(c[f], 7, 0)))
+        ahead = [t1[at_slab(p + 1), f] for f in range(4)]
+        ahead_up, c_on = rolled(ahead, 120), rolled(c, 8)
+        phm = [jnp.where(first, a, b) for a, b in zip(phm_far, c_on)]
+        php = [jnp.where(last, a, b) for a, b in zip(ahead_up, c_up)]
+        below = rolled([hth[0, big, f] for f in range(4)], lax.rem(128 - j, 128))
+        above = rolled([hth[1, big, f] for f in range(4)], 7 - j)
+        thm = [jnp.where(low_th, a, b) for a, b in zip(below, rolled(c, 1))]
+        thp = [jnp.where(high_th, a, b) for a, b in zip(above, rolled(c, 127))]
+        below = [jnp.broadcast_to(hr2[0, q, pl.ds(f, 1), :], (8, 128)) for f in range(4)]
+        above = [jnp.broadcast_to(hr2[1, q, pl.ds(f, 1), :], (8, 128)) for f in range(4)]
+        rm = [jnp.where(low_r, a, b) for a, b in zip(below, rolled(c, 1, 0))]
+        rp = [jnp.where(high_r, a, b) for a, b in zip(above, rolled(c, 7, 0))]
         new = updated(c, ((2, phm), (3, thm), (1, rm)), ((2, php), (3, thp), (1, rp)))
-        return turn(new)
+        return turn(new), (ahead, c_on, ahead_up)
 
     def rho_message(p):
         return remote(fin.at[p, 0], rho_back.at[phi], rs, rr, {"phi": p})
@@ -299,6 +322,13 @@
 
     own_rho = pltpu.make_async_copy(fin.at[phi, 0], rho_back.at[phi], ls.at[1])
     own_vel = pltpu.make_async_copy(fin.at[phi, pl.ds(1, 3)], back.at[phi], ls.at[2])
+
+    def send_far(zoff, message):
+        def one_slab(i, c):
+            message(lax.rem(z + zoff, 8) * 8 + i).start()
+            return c
+
+        lax.fori_loop(0, 8, one_slab, 0, unroll=2)
 
     def send(zoff, message, own_message):
         def one_slab(i, c):
@@ -319,29 +349,31 @@
     def block(i, carry):
         start = lax.rem(z + spread(i), 8) * 8
 
-        def slab(k, prev):
-            cur = hydro_slab(start + k)
+        def slab(k, carry):
+            prev, window = carry
+            cur, window = hydro_slab(start + k, window)
             out = blend(cur, prev)
             for f in range(4):
                 fin[start + k, f] = out[f]
-            return cur
-
-        lax.fori_loop(0, 8, slab, hydro_slab(start - 1), unroll=UNROLL)
+            return cur, window
+
+        lax.fori_loop(0, 8, slab, hydro_slab(start - 1, enter(start - 1)), unroll=UNROLL)
 
         @pl.when(i > 0)
         def _():
-            send(spread(i - 1), rho_message, own_rho)
+            send_far(spread(i - 1), rho_message)
 
         @pl.when(i == 5)
         def _():
-            send(4, vel_message, own_vel)
+            send_far(4, vel_message)
 
         return carry
 
     lax.fori_loop(0, 8, block, 0)
     send(0, rho_message, own_rho)
-    for off in (1, 7, 0):
-        send(off, vel_message, own_vel)
+    send_far(1, vel_message)
+    send_far(7, vel_message)
+    send(0, vel_message, own_vel)
 
     wait_all(rho_back.at[pl.ds(0, 63)], (rs, rr))
     own_rho.wait()
@@ -382,7 +414,7 @@
                 over(n, end).start()
 
     for off in (3, 5, 2, 6):
-        send(off, vel_message, own_vel)
+        send_far(off, vel_message)
     for n in (1, 2, 3):
         up(n).wait()
     own_light.wait()
@@ -530,20 +562,24 @@
         weight = jnp.where((k >= 0) & (k < 128), weight, 0.0)
         k = jnp.clip(k, 0, 127)
 
-        def tiles(i, total):
-            base = (lo + i) * 8
-            near = lo + i - first_tile
+        def tile(near, total):
+            shifted = v - ((near + first_tile) * 8).astype(F32)
             slab = jnp.where(near < 0, 32, jnp.where(near > 63, 33, near // 2 % 8 * 4 + near // 16))
             start = pl.multiple_of(slab * 16 + (near + 2) % 2 * 8, 8)
             block = w_ref[q, pl.ds(start, 8), :]
-            shifted = v - base.astype(F32)
             for s in range(8):
                 line = jnp.broadcast_to(block[s : s + 1, :], (8, 128))
                 got = jnp.take_along_axis(line, k, axis=1, mode="promise_in_bounds")
                 total = total + jnp.maximum(1.0 - jnp.abs(shifted - float(s)), 0.0) * got
             return total
 
-        total = lax.fori_loop(0, count, tiles, jnp.zeros((8, 128), F32))
+        def pair(i, totals):
+            near = lo - first_tile + 2 * i
+            return tile(near, totals[0]), tile(near + 1, totals[1])
+
+        nothing = jnp.zeros((8, 128), F32)
+        even, odd = lax.fori_loop(0, (count + 1) // 2, pair, (nothing, nothing))
+        total = even + odd
         acc[:, cols] = acc[:, cols] + weight * total
         return carry
 
@@ -558,13 +594,13 @@
     one = pltpu.SemaphoreType.DMA
     back, table, rho_back, upos, vpos = pl.pallas_call(
         main_kernel, name="main", out_shape=(sds(64, 3, 8, 128), sds(4, 9, 4, 16, 128), sds(64, 8, 128), sds(8, 1024), sds(8, 1024)),
-        in_specs=[SM, SM, VM, VM], out_specs=(ANY, ANY, VM, VM, VM),
+        in_specs=[SM, SM, ANY, ANY], out_specs=(ANY, ANY, VM, VM, VM),
         scratch_shapes=[
-            vmem(4, 4, 144, 128), vmem(2, 16, 128), vmem(2, 4, 32, 128), vmem(2, 16, 128), vmem(2, 128, 128),
+            vmem(16, 32, 128), vmem(3, 16, 32, 128), vmem(4, 4, 144, 128), vmem(2, 16, 128), vmem(2, 4, 32, 128), vmem(2, 16, 128), vmem(2, 128, 128),
             vmem(64, 4, 8, 128), vmem(64, 4, 8, 128), vmem(64, 4, 8, 128),
             vmem(2, 8, 4, 8, 128), vmem(2, 64, 4, 128), vmem(2, 8, 4, 8, 128), vmem(2, 64, 4, 128),
             vmem(64, 4, 8, 128), vmem(512, 128), vmem(16, 128),
-            dma(6), dma(6), one, one, dma(4), dma(4), one, one, one, one, dma(4), dma(8), dma(8),
+            dma(6), dma(6), one, one, dma(4), dma(4), one, one, one, one, dma(6), dma(8), dma(8),
             dma(32), dma(32), dma(16), dma(16), dma(16), dma(16),
         ],
         compiler_params=pltpu.CompilerParams(collective_id=0, has_side_effects=True),

time: 97.3 us -> 94.6 us (0.972)
  Pallas kernels: 95.9 us -> 93.4 us
    pallas_call x1, Pallas kernels: 9.58 us -> 8.07 us  [body(): pl.pallas_call(functools.partial(last_kernel, most=most), name='last', ou...]
    pallas_call x1, Pallas kernels: 86.3 us -> 85.3 us  [body(): pl.pallas_call(main_kernel, name='main', out_shape=(sds(64, 3, 8, 128), s...]
where the time goes in v4:
time: 94.6 us; the launch traced here: 94 us
  Pallas kernels  93.4 us (99%)
    pallas_call x1, Pallas kernels, body(): pl.pallas_call(main_kernel, name='main', out_shape=(sds(64, 3, 8, 128), s...  85.3 us
    pallas_call x1, Pallas kernels, body(): pl.pallas_call(functools.partial(last_kernel, most=most), name='last', ou...  8.07 us

profile of v4, /device:TPU:77, one launch (start us, length us, event | category | flops | bytes accessed | tf_op | source)
XLA Modules:
  0.0 94.0 jit_solution(4276335431014193135)
XLA Ops:
  0.6 85.3 %main.1 = (f32[64,3,8,128]{3,2,1,0:T(8,128)}, f32[4,9,4,16,128]{4,3,2,1,0:T(8,128)}, f32[64,8,128]{2,1,0:T(8,128)}, f32[8,1024]{1,0:T(8,128)}, f32[8,1024]{1,0:T(8,128)}) custom-call(s32[16]{0:T(128)} %shift_ref.1, f32[16]{0:T(128)} %frac_ref.1, f32[16,32,128]{2,1,0:T(8,128)} %rho_in.1, f32[3,16,32,128]{3,2,1,0:T(8,128)} %vel_in.1), custom_call_target="tpu_custom_call" | custom-call | tf_op jit(solution)/shard_map/main/pallas_call | solution.py:595
  86.0 8.1 %last.1 = (f32[16,32,128]{2,1,0:T(8,128)}, f32[3,16,32,128]{3,2,1,0:T(8,128)}, f32[4,1024]{1,0:T(4,128)}) custom-call(s32[4096]{0:T(1024)} %constant.2.clone.plan_ref, f32[8,1024]{1,0:T(8,128)} %get-tuple-element.8.u_ref, f32[8,1024]{1,0:T(8,128)} %get-tuple-element.9.v_ref, f32[64,8,128]{2,1,0:T(8,128)} %get-tuple-element.10.rho_src, ...), custom_call_target="tpu_custom_call" | custom-call | tf_op jit(solution)/shard_map/last/pallas_call | solution.py:611

commit v5 on v4

--- a/solution.py
+++ b/solution.py
@@ -77,7 +77,7 @@
 def main_kernel(
     shift_ref, frac_ref, rho_in, vel_in, back, table, rho_back, u_ref, v_ref,
     rho_ref, vel_ref, pad, edge, hphi, hr, ht, stepped, cyc, t1, th_edge, r_edge, hth, hr2, fin, flat, light,
-    es, er, as_, ar, bs, br, rs, rr, vs, vr, ls, us, ur, hs, hrr, ps, pr, gs, gr,
+    word, es, er, as_, ar, bs, br, rs, rr, vs, vr, ls, us, ur, hs, hrr, ps, pr, gs, gr,
 ):
     phi, row = lax.axis_index("phi"), lax.axis_index("row")
     z, x, y = phi // 8, lax.rem(phi // 2, 4), lax.rem(phi, 2)
@@ -109,23 +109,24 @@
     for c in loads:
         c.start()
 
-    def greet_phi(i, c):
-        peer = lax.rem(z + spread(i // 8), 8) * 8 + lax.rem(i, 8)
-
-        @pl.when(peer != phi)
-        def _():
-            signal({"phi": peer})
-
+    def plane(d):
+        return {"phi": z * 8 + lax.rem(xy + d, 8)}
+
+    def beyond(d):
+        return {"phi": lax.rem(z + d, 8) * 8 + xy}
+
+    def greet_plane(d, c):
+        signal(plane(d))
         return c
 
     def greet_chip(n, c):
         signal(chip(n))
         return c
 
-    lax.fori_loop(0, 64, greet_phi, 0)
-    for peer in (row_low, row_high, band_low, band_high, sibling):
+    for peer in (phi_low, phi_high, row_low, row_high, band_low, band_high, beyond(1), beyond(7), sibling):
         signal(peer)
     lax.fori_loop(1, 16, greet_chip, 0)
+    lax.fori_loop(1, 8, greet_plane, 0)
 
     for c in loads:
         c.wait()
@@ -136,7 +137,7 @@
             pad[f, g, 8:136, :] = t
             edge[0, pl.ds(f * 4 + g, 1), :] = t[0:1, :]
             edge[1, pl.ds(f * 4 + g, 1), :] = t[127:128, :]
-    pl.semaphore_wait(pltpu.get_barrier_semaphore(), 83)
+    pl.semaphore_wait(pltpu.get_barrier_semaphore(), 31)
     copies = [
         remote(rho_ref.at[15], hphi.at[0, 0], es.at[0], er.at[0], phi_high),
         remote(vel_ref.at[:, 15], hphi.at[0, pl.ds(1, 3)], es.at[1], er.at[1], phi_high),
@@ -147,6 +148,10 @@
     ]
     for c in copies:
         c.start()
+    for i, d in enumerate((1, 2, 2)):
+        for peer in (beyond(d), beyond(8 - d)):
+            pl.semaphore_signal(word.at[i], inc=1, device_id=peer, device_id_type=MESH)
+        pl.semaphore_wait(word.at[i], 2)
     for c in copies:
         c.wait()
     has_low = jnp.where(row > 0, 1.0, 0.0)
@@ -256,7 +261,22 @@
         for f in range(4):
             th_edge[0, big, f] = bottom[f]
             th_edge[1, big, f] = top[f]
+
+        @pl.when((big > 0) & (big % 2 == 0))
+        def _():
+            for c in edge_copies(big // 2 - 1, 1):
+                c.start()
+
         return prev
+
+    def edge_copies(piece, count):
+        slabs, groups = pl.ds(piece * 16, 16 * count), pl.ds(piece * 2, 2 * count)
+        return [
+            remote(r_edge.at[1, slabs], hr2.at[0, slabs], bs.at[0], br.at[0], band_high),
+            remote(r_edge.at[0, slabs], hr2.at[1, slabs], bs.at[1], br.at[1], band_low),
+            remote(th_edge.at[1, groups], hth.at[0, groups], bs.at[2], br.at[2], group_high),
+            remote(th_edge.at[0, groups], hth.at[1, groups], bs.at[3], br.at[3], group_low),
+        ]
 
     pixel = (phi * 4 + row) * 4 + lax.broadcasted_iota(jnp.int32, (8, 1024), 0) % 4
     column = lax.broadcasted_iota(jnp.int32, (8, 1024), 1)
@@ -269,15 +289,9 @@
     wait_all(cyc.at[pl.ds(0, 63)], (as_, ar))
     own.wait()
     lax.fori_loop(0, 8, move, cycle_slab(-1))
-    copies = [
-        remote(r_edge.at[1], hr2.at[0], bs.at[0], br.at[0], band_high),
-        remote(r_edge.at[0], hr2.at[1], bs.at[1], br.at[1], band_low),
-        remote(th_edge.at[1], hth.at[0], bs.at[2], br.at[2], group_high),
-        remote(th_edge.at[0], hth.at[1], bs.at[3], br.at[3], group_low),
-    ]
-    for c in copies:
+    for c in edge_copies(3, 1):
         c.start()
-    for c in copies:
+    for c in edge_copies(0, 4):
         c.wait()
     for side_of, cond in enumerate((band > 0, band < 63)):
         hr2[side_of] = hr2[side_of] * jnp.where(cond, 1.0, 0.0)
@@ -566,20 +580,19 @@
             shifted = v - ((near + first_tile) * 8).astype(F32)
             slab = jnp.where(near < 0, 32, jnp.where(near > 63, 33, near // 2 % 8 * 4 + near // 16))
             start = pl.multiple_of(slab * 16 + (near + 2) % 2 * 8, 8)
-            block = w_ref[q, pl.ds(start, 8), :]
             for s in range(8):
-                line = jnp.broadcast_to(block[s : s + 1, :], (8, 128))
+                line = jnp.broadcast_to(w_ref[q, pl.ds(start + s, 1), :], (8, 128))
                 got = jnp.take_along_axis(line, k, axis=1, mode="promise_in_bounds")
                 total = total + jnp.maximum(1.0 - jnp.abs(shifted - float(s)), 0.0) * got
             return total
 
         def pair(i, totals):
-            near = lo - first_tile + 2 * i
-            return tile(near, totals[0]), tile(near + 1, totals[1])
+            near = lo - first_tile + 4 * i
+            return tuple(tile(near + i, t) for i, t in enumerate(totals))
 
         nothing = jnp.zeros((8, 128), F32)
-        even, odd = lax.fori_loop(0, (count + 1) // 2, pair, (nothing, nothing))
-        total = even + odd
+        a, b, c, d = lax.fori_loop(0, (count + 3) // 4, pair, (nothing,) * 4)
+        total = (a + b) + (c + d)
         acc[:, cols] = acc[:, cols] + weight * total
         return carry
 
@@ -600,7 +613,7 @@
             vmem(64, 4, 8, 128), vmem(64, 4, 8, 128), vmem(64, 4, 8, 128),
             vmem(2, 8, 4, 8, 128), vmem(2, 64, 4, 128), vmem(2, 8, 4, 8, 128), vmem(2, 64, 4, 128),
             vmem(64, 4, 8, 128), vmem(512, 128), vmem(16, 128),
-            dma(6), dma(6), one, one, dma(4), dma(4), one, one, one, one, dma(6), dma(8), dma(8),
+            pltpu.SemaphoreType.REGULAR((3,)), dma(6), dma(6), one, one, dma(4), dma(4), one, one, one, one, dma(6), dma(8), dma(8),
             dma(32), dma(32), dma(16), dma(16), dma(16), dma(16),
         ],
         compiler_params=pltpu.CompilerParams(collective_id=0, has_side_effects=True),

time: 94.6 us -> 91 us (0.962)
  Pallas kernels: 93.4 us -> 89 us
    pallas_call x1, Pallas kernels: 85.3 us -> 81.7 us  [body(): pl.pallas_call(main_kernel, name='main', out_shape=(sds(64, 3, 8, 128), s...]
where the time goes in v5:
time: 91 us; the launch traced here: 89.7 us
  Pallas kernels  89 us (98%)
    pallas_call x1, Pallas kernels, body(): pl.pallas_call(main_kernel, name='main', out_shape=(sds(64, 3, 8, 128), s...  81.7 us
    pallas_call x1, Pallas kernels, body(): pl.pallas_call(functools.partial(last_kernel, most=most), name='last', ou...  7.32 us

profile of v5, /device:TPU:77, one launch (start us, length us, event | category | flops | bytes accessed | tf_op | source)
XLA Modules:
  0.0 89.7 jit_solution(17118866791940423785)
XLA Ops:
  0.6 81.7 %main.1 = (f32[64,3,8,128]{3,2,1,0:T(8,128)}, f32[4,9,4,16,128]{4,3,2,1,0:T(8,128)}, f32[64,8,128]{2,1,0:T(8,128)}, f32[8,1024]{1,0:T(8,128)}, f32[8,1024]{1,0:T(8,128)}) custom-call(s32[16]{0:T(128)} %shift_ref.1, f32[16]{0:T(128)} %frac_ref.1, f32[16,32,128]{2,1,0:T(8,128)} %rho_in.1, f32[3,16,32,128]{3,2,1,0:T(8,128)} %vel_in.1), custom_call_target="tpu_custom_call" | custom-call | tf_op jit(solution)/shard_map/main/pallas_call | solution.py:608
  82.3 7.3 %last.1 = (f32[16,32,128]{2,1,0:T(8,128)}, f32[3,16,32,128]{3,2,1,0:T(8,128)}, f32[4,1024]{1,0:T(4,128)}) custom-call(s32[4096]{0:T(1024)} %constant.2.clone.plan_ref, f32[8,1024]{1,0:T(8,128)} %get-tuple-element.8.u_ref, f32[8,1024]{1,0:T(8,128)} %get-tuple-element.9.v_ref, f32[64,8,128]{2,1,0:T(8,128)} %get-tuple-element.10.rho_src, ...), custom_call_target="tpu_custom_call" | custom-call | tf_op jit(solution)/shard_map/last/pallas_call | solution.py:624

commit v6 on v5

--- a/solution.py
+++ b/solution.py
@@ -46,13 +46,16 @@
     return out
 
 
-def updated(here, lower, upper):
+def pushed(here, lower, upper):
     total = None
     for (comp, low), (_, high) in zip(lower, upper):
         p, m = side(low, comp, 0.75), side(high, comp, -0.75)
         part = [b - a for a, b in zip(p, m)]
         total = part if total is None else [s + t for s, t in zip(total, part)]
-    new = [0.775 * c - 0.05 * t for c, t in zip(conserved(here), total)]
+    return [0.775 * c - 0.05 * t for c, t in zip(conserved(here), total)]
+
+
+def primitive(new):
     inv = 1.0 / new[0]
     return [new[0], new[1] * inv, new[2] * inv, new[3] * inv]
 
@@ -207,7 +210,7 @@
             above = [pltpu.roll(side_edge[f // 2], (120 - offs[f] - 32) % 128, 1) for f in range(4)]
             phm = [jnp.where(first, lo, t) for lo, t in zip(below, rolled(c, 8))]
             php = [jnp.where(last, hi, t) for hi, t in zip(above, rolled(c, 120))]
-            new = updated(c, ((2, phm), (3, thm), (1, before)), ((2, php), (3, thp), (1, after)))
+            new = primitive(pushed(c, ((2, phm), (3, thm), (1, before)), ((2, php), (3, thp), (1, after))))
             d = spot(i, g)
             for f in range(4):
                 stepped[d, f] = new[f]
@@ -291,6 +294,28 @@
     lax.fori_loop(0, 8, move, cycle_slab(-1))
     for c in edge_copies(3, 1):
         c.start()
+    sub = lax.broadcasted_iota(jnp.int32, (8, 128), 0)
+    low_r, high_r = sub == 0, sub == 7
+
+    def inside(q, window):
+        c, phm_far, c_up = window
+        ahead = [t1[lax.rem(q + 1, 64), f] for f in range(4)]
+        ahead_up, c_on = rolled(ahead, 120), rolled(c, 8)
+        phm = [jnp.where(first, a, b) for a, b in zip(phm_far, c_on)]
+        php = [jnp.where(last, a, b) for a, b in zip(ahead_up, c_up)]
+        thm = [jnp.where(low_th, 0.0, b) for b in rolled(c, 1)]
+        thp = [jnp.where(high_th, 0.0, b) for b in rolled(c, 127)]
+        rm = [jnp.where(low_r, 0.0, b) for b in rolled(c, 1, 0)]
+        rp = [jnp.where(high_r, 0.0, b) for b in rolled(c, 7, 0)]
+        new = pushed(c, ((2, phm), (3, thm), (1, rm)), ((2, php), (3, thp), (1, rp)))
+        for f in range(4):
+            stepped[q, f] = new[f]
+        return ahead, c_on, ahead_up
+
+    here = [t1[0, f] for f in range(4)]
+    lax.fori_loop(
+        0, 64, inside, (here, rolled([t1[63, f] for f in range(4)], 8), rolled(here, 120)), unroll=UNROLL
+    )
     for c in edge_copies(0, 4):
         c.wait()
     for side_of, cond in enumerate((band > 0, band < 63)):
@@ -298,35 +323,21 @@
     for side_of, cond in enumerate((x > 0, x < 3)):
         hth[side_of] = hth[side_of] * jnp.where(cond, 1.0, 0.0)
 
-    sub = lax.broadcasted_iota(jnp.int32, (8, 128), 0)
-    low_r, high_r = sub == 0, sub == 7
-
-    def at_slab(p):
-        return lax.rem(p + 192 - whole, 64)
-
-    def enter(p):
-        here = [t1[at_slab(p), f] for f in range(4)]
-        behind = rolled([t1[at_slab(p - 1), f] for f in range(4)], 8)
-        return here, behind, rolled(here, 120)
-
-    def hydro_slab(p, window):
-        c, phm_far, c_up = window
-        q = at_slab(p)
+    offset_r, offset_th = jnp.where(low_r, 0.75, -0.75), jnp.where(low_th, 0.75, -0.75)
+    weight_r = jnp.where(low_r, 0.05, jnp.where(high_r, -0.05, 0.0))
+    weight_th = jnp.where(low_th, 0.05, jnp.where(high_th, -0.05, 0.0))
+
+    def hydro_slab(p):
+        q = lax.rem(p + 192 - whole, 64)
         big, j = q // 8, lax.rem(q, 8)
-        ahead = [t1[at_slab(p + 1), f] for f in range(4)]
-        ahead_up, c_on = rolled(ahead, 120), rolled(c, 8)
-        phm = [jnp.where(first, a, b) for a, b in zip(phm_far, c_on)]
-        php = [jnp.where(last, a, b) for a, b in zip(ahead_up, c_up)]
         below = rolled([hth[0, big, f] for f in range(4)], lax.rem(128 - j, 128))
         above = rolled([hth[1, big, f] for f in range(4)], 7 - j)
-        thm = [jnp.where(low_th, a, b) for a, b in zip(below, rolled(c, 1))]
-        thp = [jnp.where(high_th, a, b) for a, b in zip(above, rolled(c, 127))]
+        add_th = side([jnp.where(low_th, a, b) for a, b in zip(below, above)], 3, offset_th)
         below = [jnp.broadcast_to(hr2[0, q, pl.ds(f, 1), :], (8, 128)) for f in range(4)]
         above = [jnp.broadcast_to(hr2[1, q, pl.ds(f, 1), :], (8, 128)) for f in range(4)]
-        rm = [jnp.where(low_r, a, b) for a, b in zip(below, rolled(c, 1, 0))]
-        rp = [jnp.where(high_r, a, b) for a, b in zip(above, rolled(c, 7, 0))]
-        new = updated(c, ((2, phm), (3, thm), (1, rm)), ((2, php), (3, thp), (1, rp)))
-        return turn(new), (ahead, c_on, ahead_up)
+        add_r = side([jnp.where(low_r, a, b) for a, b in zip(below, above)], 1, offset_r)
+        new = [stepped[q, f] + weight_th * add_th[f] + weight_r * add_r[f] for f in range(4)]
+        return turn(primitive(new))
 
     def rho_message(p):
         return remote(fin.at[p, 0], rho_back.at[phi], rs, rr, {"phi": p})
@@ -363,21 +374,20 @@
     def block(i, carry):
         start = lax.rem(z + spread(i), 8) * 8
 
-        def slab(k, carry):
-            prev, window = carry
-            cur, window = hydro_slab(start + k, window)
+        def slab(k, prev):
+            cur = hydro_slab(start + k)
             out = blend(cur, prev)
             for f in range(4):
                 fin[start + k, f] = out[f]
-            return cur, window
-
-        lax.fori_loop(0, 8, slab, hydro_slab(start - 1, enter(start - 1)), unroll=UNROLL)
+            return cur
+
+        lax.fori_loop(0, 8, slab, hydro_slab(start - 1), unroll=8)
 
         @pl.when(i > 0)
         def _():
             send_far(spread(i - 1), rho_message)
 
-        @pl.when(i == 5)
+        @pl.when(i == 3)
         def _():
             send_far(4, vel_message)
 

time: 91 us -> 89.1 us (0.979)
  Pallas kernels: 89 us -> 87.7 us
    pallas_call x1, Pallas kernels: 81.7 us -> 80.3 us  [body(): pl.pallas_call(main_kernel, name='main', out_shape=(sds(64, 3, 8, 128), s...]
where the time goes in v6:
time: 89.1 us; the launch traced here: 88.3 us
  Pallas kernels  87.7 us (98%)
    pallas_call x1, Pallas kernels, body(): pl.pallas_call(main_kernel, name='main', out_shape=(sds(64, 3, 8, 128), s...  80.3 us
    pallas_call x1, Pallas kernels, body(): pl.pallas_call(functools.partial(last_kernel, most=most), name='last', ou...  7.32 us

profile of v6, /device:TPU:77, one launch (start us, length us, event | category | flops | bytes accessed | tf_op | source)
XLA Modules:
  0.0 88.3 jit_solution(17172981178834066475)
XLA Ops:
  0.6 80.3 %main.1 = (f32[64,3,8,128]{3,2,1,0:T(8,128)}, f32[4,9,4,16,128]{4,3,2,1,0:T(8,128)}, f32[64,8,128]{2,1,0:T(8,128)}, f32[8,1024]{1,0:T(8,128)}, f32[8,1024]{1,0:T(8,128)}) custom-call(s32[16]{0:T(128)} %shift_ref.1, f32[16]{0:T(128)} %frac_ref.1, f32[16,32,128]{2,1,0:T(8,128)} %rho_in.1, f32[3,16,32,128]{3,2,1,0:T(8,128)} %vel_in.1), custom_call_target="tpu_custom_call" | custom-call | tf_op jit(solution)/shard_map/main/pallas_call | solution.py:618
  81.0 7.3 %last.1 = (f32[16,32,128]{2,1,0:T(8,128)}, f32[3,16,32,128]{3,2,1,0:T(8,128)}, f32[4,1024]{1,0:T(4,128)}) custom-call(s32[4096]{0:T(1024)} %constant.2.clone.plan_ref, f32[8,1024]{1,0:T(8,128)} %get-tuple-element.8.u_ref, f32[8,1024]{1,0:T(8,128)} %get-tuple-element.9.v_ref, f32[64,8,128]{2,1,0:T(8,128)} %get-tuple-element.10.rho_src, ...), custom_call_target="tpu_custom_call" | custom-call | tf_op jit(solution)/shard_map/last/pallas_call | solution.py:634

commit v7 on v6

--- a/solution.py
+++ b/solution.py
@@ -14,7 +14,7 @@
 NPHI = 1024
 NR = 512
 NTH = 32
-UNROLL = 4
+UNROLL = 8
 KAPPA = 1.5
 R_INNER = 0.2
 F32 = jnp.float32
@@ -387,7 +387,7 @@
         def _():
             send_far(spread(i - 1), rho_message)
 
-        @pl.when(i == 3)
+        @pl.when(i == 2)
         def _():
             send_far(4, vel_message)
 

time: 89.1 us -> 89.2 us (level)
  no operation moved by 1% of the time
where the time goes in v7:
time: 89.2 us; the launch traced here: 88.5 us
  Pallas kernels  87.9 us (99%)
    pallas_call x1, Pallas kernels, body(): pl.pallas_call(main_kernel, name='main', out_shape=(sds(64, 3, 8, 128), s...  80.6 us
    pallas_call x1, Pallas kernels, body(): pl.pallas_call(functools.partial(last_kernel, most=most), name='last', ou...  7.32 us

profile of v7, /device:TPU:77, one launch (start us, length us, event | category | flops | bytes accessed | tf_op | source)
XLA Modules:
  0.0 88.5 jit_solution(5437950889202631909)
XLA Ops:
  0.6 80.6 %main.1 = (f32[64,3,8,128]{3,2,1,0:T(8,128)}, f32[4,9,4,16,128]{4,3,2,1,0:T(8,128)}, f32[64,8,128]{2,1,0:T(8,128)}, f32[8,1024]{1,0:T(8,128)}, f32[8,1024]{1,0:T(8,128)}) custom-call(s32[16]{0:T(128)} %shift_ref.1, f32[16]{0:T(128)} %frac_ref.1, f32[16,32,128]{2,1,0:T(8,128)} %rho_in.1, f32[3,16,32,128]{3,2,1,0:T(8,128)} %vel_in.1), custom_call_target="tpu_custom_call" | custom-call | tf_op jit(solution)/shard_map/main/pallas_call | solution.py:618
  81.2 7.3 %last.1 = (f32[16,32,128]{2,1,0:T(8,128)}, f32[3,16,32,128]{3,2,1,0:T(8,128)}, f32[4,1024]{1,0:T(4,128)}) custom-call(s32[4096]{0:T(1024)} %constant.2.clone.plan_ref, f32[8,1024]{1,0:T(8,128)} %get-tuple-element.8.u_ref, f32[8,1024]{1,0:T(8,128)} %get-tuple-element.9.v_ref, f32[64,8,128]{2,1,0:T(8,128)} %get-tuple-element.10.rho_src, ...), custom_call_target="tpu_custom_call" | custom-call | tf_op jit(solution)/shard_map/last/pallas_call | solution.py:634
